TPU v7x, 32 devices: a whole 2x2x4 slice. The times are simulated.
32 devices in a mesh: section: 2 (over core), dp: 16 (over z, y, x).
Axes of the slice: x: 2, y: 2, z: 4, core: 2. Of those that a mesh axis runs over, the one named last changes fastest.
Arguments:
- tokens: bfloat16 [32, 128, 1536], P('dp'), may hold values from -6 to 6
- cotangent: bfloat16 [32, 128, 1536], P('dp'), may hold values from -6 to 6
- segments: int32 [32, 128], P('dp'), may hold values from 0 to 2, never falling along the last dimension, each value on 1 to 64 neighbouring positions
- gain_attn: bfloat16 [2, 1536], P('section', 'dp'), may hold values from 0.099609375 to 1.8984375
- w_qkv: bfloat16 [2, 1536, 3072], P('section', 'dp'), may hold values from -0.15625 to 0.15625
- w_out: bfloat16 [2, 1536, 1536], P('section', 'dp'), may hold values from -0.875 to 0.875
- gain_mlp: bfloat16 [2, 1536], P('section', 'dp'), may hold values from 0.099609375 to 1.8984375
- w_gate_up: bfloat16 [2, 1536, 8192], P('section', 'dp'), may hold values from -0.15625 to 0.15625
- w_down: bfloat16 [2, 4096, 1536], P('section', 'dp'), may hold values from -0.1875 to 0.1875
Outputs:
- activations: bfloat16 [2, 32, 128, 1536], P('section', 'dp')
- input_grads: float32 [2, 32, 128, 1536], P('section', 'dp')
- grad_gain_attn: float32 [2, 1536], P('section', 'dp')
- grad_w_qkv: float32 [2, 1536, 3072], P('section', 'dp')
- grad_w_out: float32 [2, 1536, 1536], P('section', 'dp')
- grad_gain_mlp: float32 [2, 1536], P('section', 'dp')
- grad_w_gate_up: float32 [2, 1536, 8192], P('section', 'dp')
- grad_w_down: float32 [2, 4096, 1536], P('section', 'dp')
Inputs may be any that keep to these rules, and one draw needn't show every extreme that they name: `segments`: along each sequence the segment numbers never fall; one segment covers at most 64 positions of a sequence.
All inputs are finite; a program needn't handle non-finite values.
Results may differ from a plain program's by a relative error of at most 0.025.
Values may be sent and summed in bfloat16 or wider, within the bound.
No kernel may reach another device: no remote copies, remote signals or barrier semaphores. Data moves between devices by JAX's collectives and lax.ppermute only.
A program may use at most 576 MiB of HBM per device.

v0:
```python
import jax
import jax.numpy as jnp
from jax import lax
from jax.sharding import PartitionSpec as P

HEADS = 16
KV_HEADS = 8
HEAD_WIDTH = 96
FF = 4096


rms_eps = 1e-05
rope_base = 10000.0


def shifted(value, axis, steps):
    count = lax.axis_size(axis)
    initial, last = (max(0, -steps), min(count, count - steps))
    return lax.ppermute(value, axis, [(source, source + steps) for source in range(initial, last)])


def dot_tn(left, right):
    return lax.dot_general(
        left, right, (((0,), (0,)), ((), ())), preferred_element_type=jnp.float32
    )


def dot_nt(left, right):
    return lax.dot_general(
        left, right, (((1,), (1,)), ((), ())), preferred_element_type=jnp.float32
    )


def rms_scale(value):
    return lax.rsqrt(jnp.mean(value * value, axis=-1, keepdims=True) + rms_eps)


def rotary(labels):
    length = labels.shape[0]
    same_doc = labels[:, None] == labels[None, :]
    indices = jnp.arange(length)
    before = indices[None, :] < indices[:, None]
    places = jnp.sum(jnp.where(same_doc & before, 1, 0), axis=1).astype(jnp.float32)
    half_dim = HEAD_WIDTH // 2
    frequency = rope_base ** (-jnp.arange(half_dim, dtype=jnp.float32) / half_dim)
    angles = places[:, None] * frequency[None, :]
    allowed = same_doc & (indices[None, :] <= indices[:, None])
    return (jnp.cos(angles), jnp.sin(angles), allowed)


def rotate(heads, cos_table, sin_table):
    half_dim = heads.shape[-1] // 2
    front_half = heads[..., :half_dim]
    back_half = heads[..., half_dim:]
    cosine = cos_table[:, None, :]
    sine_rows = sin_table[:, None, :]
    return jnp.concatenate(
        [front_half * cosine - back_half * sine_rows, back_half * cosine + front_half * sine_rows],
        axis=-1,
    )


def norm_back(value, scale_rows, gain_row, incoming):
    unit_rows = value * scale_rows
    grad_gain = jnp.sum(incoming * unit_rows, axis=0)
    grad_unit = incoming * gain_row.astype(jnp.float32)
    grad_value = scale_rows * (
        grad_unit - unit_rows * jnp.mean(grad_unit * unit_rows, axis=-1, keepdims=True)
    )
    return (grad_value, grad_gain)


def attention_scores(query_rows, key_head_rows, allowed):
    logit_scores = jnp.einsum(
        "yamf,naf->amyn", query_rows, key_head_rows, preferred_element_type=jnp.float32
    ) * HEAD_WIDTH ** (-0.5)
    return jnp.where(allowed[None, None], logit_scores, -1e30)


def forward_layer(hidden, labels, weights):
    gain_one, w_qkv, w_out, gain_two, w_gate_up, w_down = weights
    length = hidden.shape[0]
    group_size = HEADS // KV_HEADS
    cos_table, sin_table, allowed = rotary(labels)
    scale_one = rms_scale(hidden)
    normed = (hidden * scale_one * gain_one.astype(jnp.float32)).astype(jnp.bfloat16)
    joined = jnp.dot(normed, w_qkv, preferred_element_type=jnp.float32)
    split_q = HEADS * HEAD_WIDTH
    split_k = split_q + KV_HEADS * HEAD_WIDTH
    query_rows = rotate(
        joined[:, :split_q].reshape(length, HEADS, HEAD_WIDTH), cos_table, sin_table
    )
    query_rows = query_rows.astype(jnp.bfloat16).reshape(length, KV_HEADS, group_size, HEAD_WIDTH)
    key_head_rows = rotate(
        joined[:, split_q:split_k].reshape(length, KV_HEADS, HEAD_WIDTH), cos_table, sin_table
    ).astype(jnp.bfloat16)
    value_rows = joined[:, split_k:].reshape(length, KV_HEADS, HEAD_WIDTH).astype(jnp.bfloat16)
    logit_scores = attention_scores(query_rows, key_head_rows, allowed)
    peak = jnp.max(logit_scores, axis=-1, keepdims=True)
    log_total = peak + jnp.log(jnp.sum(jnp.exp(logit_scores - peak), axis=-1, keepdims=True))
    attention_weights = jnp.exp(logit_scores - log_total).astype(jnp.bfloat16)
    merged_heads = jnp.einsum(
        "pjqc,cpu->qpju", attention_weights, value_rows, preferred_element_type=jnp.float32
    )
    merged_heads = merged_heads.reshape(length, HEADS * HEAD_WIDTH).astype(jnp.bfloat16)
    middle = hidden + jnp.dot(merged_heads, w_out, preferred_element_type=jnp.float32)
    scale_two = rms_scale(middle)
    second = (middle * scale_two * gain_two.astype(jnp.float32)).astype(jnp.bfloat16)
    gate_up = jnp.dot(second, w_gate_up, preferred_element_type=jnp.float32)
    gate_part = gate_up[:, :FF]
    up_part = gate_up[:, FF:]
    inner_act = (jax.nn.silu(gate_part) * up_part).astype(jnp.bfloat16)
    result = middle + jnp.dot(inner_act, w_down, preferred_element_type=jnp.float32)
    stored = (
        hidden,
        scale_one,
        normed,
        query_rows,
        key_head_rows,
        value_rows,
        log_total,
        merged_heads,
        middle,
        scale_two,
        second,
        gate_part,
        up_part,
        inner_act,
        labels,
    )
    return (result, stored)


def backward_layer(grad_out, stored, weights, totals):
    gain_one, w_qkv, w_out, gain_two, w_gate_up, w_down = weights
    (
        hidden,
        scale_one,
        normed,
        query_rows,
        key_head_rows,
        value_rows,
        log_total,
        merged_heads,
        middle,
        scale_two,
        second,
        gate_part,
        up_part,
        inner_act,
        labels,
    ) = stored
    length = hidden.shape[0]
    cos_table, sin_table, allowed = rotary(labels)
    grad_low = grad_out.astype(jnp.bfloat16)
    grad_down = totals[5] + dot_tn(inner_act, grad_low)
    grad_inner = dot_nt(grad_low, w_down)
    sigmoid_gate = jax.nn.sigmoid(gate_part)
    grad_gate = grad_inner * up_part * sigmoid_gate * (1.0 + gate_part * (1.0 - sigmoid_gate))
    grad_up = grad_inner * gate_part * sigmoid_gate
    grad_pair = jnp.concatenate([grad_gate, grad_up], axis=1).astype(jnp.bfloat16)
    grad_gate_up = totals[4] + dot_tn(second, grad_pair)
    grad_second = dot_nt(grad_pair, w_gate_up)
    grad_mid, gain_two_grad = norm_back(middle, scale_two, gain_two, grad_second)
    grad_mid = grad_mid + grad_out
    mid_low = grad_mid.astype(jnp.bfloat16)
    grad_wout = totals[2] + dot_tn(merged_heads, mid_low)
    gradient_mixed_heads = dot_nt(mid_low, w_out).astype(jnp.bfloat16).reshape(query_rows.shape)
    logit_scores = attention_scores(query_rows, key_head_rows, allowed)
    attention_weights = jnp.exp(logit_scores - log_total)
    grad_values = jnp.einsum(
        "puew,epun->wpn",
        attention_weights.astype(jnp.bfloat16),
        gradient_mixed_heads,
        preferred_element_type=jnp.float32,
    )
    grad_probs = jnp.einsum(
        "yamf,naf->amyn", gradient_mixed_heads, value_rows, preferred_element_type=jnp.float32
    )
    row_dot = jnp.sum(grad_probs * attention_weights, axis=-1, keepdims=True)
    gradient_scores = (attention_weights * (grad_probs - row_dot)).astype(jnp.bfloat16)
    grad_queries = jnp.einsum(
        "pjqc,cpu->qpju", gradient_scores, key_head_rows, preferred_element_type=jnp.float32
    ) * HEAD_WIDTH ** (-0.5)
    grad_keys = jnp.einsum(
        "puew,epun->wpn", gradient_scores, query_rows, preferred_element_type=jnp.float32
    ) * HEAD_WIDTH ** (-0.5)
    grad_queries = rotate(
        grad_queries.reshape(length, HEADS, HEAD_WIDTH), cos_table, -sin_table
    ).reshape(length, HEADS * HEAD_WIDTH)
    grad_keys = rotate(grad_keys, cos_table, -sin_table).reshape(length, KV_HEADS * HEAD_WIDTH)
    grad_joined = jnp.concatenate(
        [grad_queries, grad_keys, grad_values.reshape(length, KV_HEADS * HEAD_WIDTH)], axis=1
    ).astype(jnp.bfloat16)
    grad_qkv = totals[1] + dot_tn(normed, grad_joined)
    grad_normed = dot_nt(grad_joined, w_qkv)
    grad_input, gain_one_grad = norm_back(hidden, scale_one, gain_one, grad_normed)
    grad_input = grad_input + grad_mid
    return (
        grad_input,
        (
            totals[0] + gain_one_grad,
            grad_qkv,
            grad_wout,
            totals[3] + gain_two_grad,
            grad_gate_up,
            grad_down,
        ),
    )


def shards(tokens, cotangent, segments, gain_attn, w_qkv, w_out, gain_mlp, w_gate_up, w_down):
    batches = tokens.shape[0]
    leading = lax.axis_index("section") == 0
    gathered = (
        lax.all_gather(gain_attn, "dp", axis=1, tiled=True),
        lax.all_gather(w_qkv, "dp", axis=1, tiled=True),
        lax.all_gather(w_out, "dp", axis=1, tiled=True),
        lax.all_gather(gain_mlp, "dp", axis=1, tiled=True),
        lax.all_gather(w_gate_up, "dp", axis=1, tiled=True),
        lax.all_gather(w_down, "dp", axis=1, tiled=True),
    )
    weights = tuple((shard_part[0] for shard_part in gathered))

    def run_forward(inputs, labels):
        return forward_layer(inputs, labels, weights)

    def skip_forward(inputs, labels):
        return jax.tree.map(jnp.zeros_like, forward_layer(inputs, labels, weights))

    incoming = jnp.zeros(tokens.shape[1:], jnp.bfloat16)
    results = []
    stored_all = []
    for moment in range(batches + 1):
        own_index = min(moment, batches - 1)
        prior_index = max(moment - 1, 0)
        inputs = jnp.where(leading, tokens[own_index], incoming).astype(jnp.float32)
        labels = jnp.where(leading, segments[own_index], segments[prior_index])
        active = jnp.where(leading, moment < batches, moment >= 1)
        result, stored = lax.cond(active, run_forward, skip_forward, inputs, labels)
        outgoing = result.astype(jnp.bfloat16)
        results.append(outgoing)
        stored_all.append(stored)
        if moment < batches:
            incoming = shifted(outgoing, "section", 1)
    activations = jnp.stack(
        [jnp.where(leading, results[index], results[index + 1]) for index in range(batches)]
    )[None]
    regathered = (
        lax.all_gather(gain_attn, "dp", axis=1, tiled=True),
        lax.all_gather(w_qkv, "dp", axis=1, tiled=True),
        lax.all_gather(w_out, "dp", axis=1, tiled=True),
        lax.all_gather(gain_mlp, "dp", axis=1, tiled=True),
        lax.all_gather(w_gate_up, "dp", axis=1, tiled=True),
        lax.all_gather(w_down, "dp", axis=1, tiled=True),
    )
    back_weights = tuple((shard_part[0] for shard_part in regathered))

    def run_back(grad_out, stored, totals):
        return backward_layer(grad_out, stored, back_weights, totals)

    def skip_back(grad_out, stored, totals):
        return (jnp.zeros_like(grad_out), totals)

    zero_totals = tuple((jnp.zeros(weight.shape, jnp.float32) for weight in back_weights))
    totals = zero_totals
    incoming_grad = jnp.zeros(tokens.shape[1:], jnp.bfloat16)
    step_grads = []
    for moment in range(batches + 1):
        late_index = max(batches - 1 - moment, 0)
        early_index = min(batches - moment, batches - 1)
        stored = jax.tree.map(
            lambda a, b: jnp.where(leading, a, b),
            stored_all[early_index],
            stored_all[late_index + 1],
        )
        grad_out = jnp.where(
            leading, incoming_grad.astype(jnp.float32), cotangent[late_index].astype(jnp.float32)
        )
        active = jnp.where(leading, moment >= 1, moment < batches)
        grad_input, totals = lax.cond(active, run_back, skip_back, grad_out, stored, totals)
        step_grads.append(grad_input)
        if moment < batches:
            incoming_grad = shifted(grad_input.astype(jnp.bfloat16), "section", -1)
    input_grads = jnp.stack(
        [
            jnp.where(leading, step_grads[batches - index], step_grads[batches - 1 - index])
            for index in range(batches)
        ]
    )[None]
    reduced = (
        lax.psum_scatter(totals[0][None], "dp", scatter_dimension=1, tiled=True),
        lax.psum_scatter(totals[1][None], "dp", scatter_dimension=1, tiled=True),
        lax.psum_scatter(totals[2][None], "dp", scatter_dimension=1, tiled=True),
        lax.psum_scatter(totals[3][None], "dp", scatter_dimension=1, tiled=True),
        lax.psum_scatter(totals[4][None], "dp", scatter_dimension=1, tiled=True),
        lax.psum_scatter(totals[5][None], "dp", scatter_dimension=1, tiled=True),
    )
    return (
        activations,
        input_grads,
        reduced[0],
        reduced[1],
        reduced[2],
        reduced[3],
        reduced[4],
        reduced[5],
    )


def solution(mesh):
    in_specs = (
        P("dp", None, None),
        P("dp", None, None),
        P("dp", None),
        P("section", "dp"),
        P("section", "dp", None),
        P("section", "dp", None),
        P("section", "dp"),
        P("section", "dp", None),
        P("section", "dp", None),
    )
    out_specs = (
        P("section", "dp", None, None),
        P("section", "dp", None, None),
        P("section", "dp"),
        P("section", "dp", None),
        P("section", "dp", None),
        P("section", "dp"),
        P("section", "dp", None),
        P("section", "dp", None),
    )
    return jax.shard_map(shards, mesh=mesh, in_specs=in_specs, out_specs=out_specs, check_vma=False)
```

profile of v0, /device:TPU:0, one launch (start us, length us, event | category | flops | bytes accessed | tf_op | source)
XLA Modules:
  0.0 2994.5 jit_solution(4870717082150723728)
XLA Ops:
  11.8 44.4 %all-reduce.2 = (bf16[1536]{0:T(1024)(128)(2,1)S(1)}, bf16[1536]{0:T(1024)(128)(2,1)S(1)}) all-reduce(bf16[1536]{0:T(1024)(128)(2,1)S(1)} %dynamic-update-slice, bf16[1536]{0:T(1024)(128)(2,1)S(1)} %dynamic-update-slice.1), channel_id=1, replica_groups=mesh['section'=2,'dp'=16] {'dp'}, use_global_device_ids=true, to_apply=%add | all-reduce | flops 3072 | bytes 12288 | tf_op jit(solution)/shard_map/squeeze | solution.py:223
  57.5 36.2 %all-gather.7.cloned.1.call-done = bf16[1,1536,1536]{2,1,0:T(8,128)(2,1)} async-done(((bf16[1,96,1536]{2,1,0:T(8,128)(2,1)}), bf16[1,1536,1536]{2,1,0:T(8,128)(2,1)}) %all-gather.7.cloned.1.call-update) | async-done | bytes 4718608 | tf_op jit(solution)/shard_map/all_gather | solution.py:218
  93.6 123.2 %all-gather.5.cloned.1.call-done = bf16[1,1536,3072]{2,1,0:T(8,128)(2,1)} async-done(((bf16[1,96,3072]{2,1,0:T(8,128)(2,1)}), bf16[1,1536,3072]{2,1,0:T(8,128)(2,1)}) %all-gather.5.cloned.1.call-update) | async-done | bytes 9437200 | tf_op jit(solution)/shard_map/all_gather | solution.py:217
  216.9 152.4 %all-gather.11.cloned.1.call-done = bf16[1,4096,1536]{2,1,0:T(8,128)(2,1)} async-done(((bf16[1,256,1536]{2,1,0:T(8,128)(2,1)}), bf16[1,4096,1536]{2,1,0:T(8,128)(2,1)}) %all-gather.11.cloned.1.call-update) | async-done | bytes 12582928 | tf_op jit(solution)/shard_map/all_gather | solution.py:221
  369.3 271.3 %all-gather.9.cloned.1.call-done = bf16[1,1536,8192]{2,1,0:T(8,128)(2,1)} async-done(((bf16[1,96,8192]{2,1,0:T(8,128)(2,1)}), bf16[1,1536,8192]{2,1,0:T(8,128)(2,1)}) %all-gather.9.cloned.1.call-update) | async-done | bytes 25165840 | tf_op jit(solution)/shard_map/all_gather | solution.py:220
  640.6 38.9 %conditional.4 = (f32[128,1536]{1,0:T(8,128)S(1)}, f32[128,1]{0,1:T(1,128)S(1)}, bf16[128,1536]{1,0:T(8,128)(2,1)S(1)}, bf16[128,8,2,96]{0,3,2,1:T(8,128)(2,1)},...) conditional(s32[]{:T(128)} %convert_element_type.309, () %tuple.64, ...), branch_computations={%region_0.1_spmd, %region_1.7_spmd.clone} | conditional | flops 6755065344 | bytes 140821376 | solution.py:240
  641.6 5.2 fusion.131
  656.8 4.2 multiply_reduce_fusion.12
  662.5 10.2 fusion.132
  672.7 2.7 multiply_convert_fusion.9
  675.5 4.1 fusion.75
  680.7 1.5 collective-permute-start
  683.5 2.0 fusion.124
  685.9 5.1 fusion.119
  696.7 3.4 multiply_reduce_fusion.19
  700.4 10.2 fusion.114
  710.6 2.6 fusion.127
  713.9 1.8 fusion.82
  715.7 3.1 collective-permute-start.1
  721.4 11.2 conditional.5
  727.1 1.6 broadcast.766
  728.7 1.6 broadcast.766.clone
  735.0 47.4 %conditional.6 = (f32[128,1536]{1,0:T(8,128)S(1)}, f32[1536]{0:T(1024)S(1)}, f32[1536,3072]{1,0:T(8,128)}, f32[1536,1536]{1,0:T(8,128)}, f32[1536]{0:T(1024)S(1)...) conditional(s32[]{:T(128)} %convert_element_type.325, () %tuple.68, (pred[128,1]{0,1:T(4,128)(4,1)S(1)}, ...), branch_computations={%region_19.20_spmd, %region_20.27_spmd} | conditional | flops 13573926912 | bytes 274734272 | solution.py:281
  738.0 8.7 broadcast_in_dim.181
  746.7 4.9 broadcast_in_dim.182
  751.6 16.3 broadcast_in_dim.183
  767.9 11.5 broadcast_in_dim.184
  783.8 2.0 bitcast_convert_fusion.4
  785.9 91.3 %collective-permute-done.2 = bf16[128,1536]{1,0:T(8,128)(2,1)S(1)} collective-permute-done((bf16[128,1536]{1,0:T(8,128)(2,1)S(1)}, bf16[128,1536]{1,0:T(8,128)(2,1)S(1)}, u32[]{:S(2)}, u32[]{:S(2)}) %collective-permute-start.2) | collective-permute-done | bytes 393248 | tf_op jit(solution)/shard_map/ppermute | solution.py:19
  877.2 11.6 multiply_convert_fusion.13
  888.8 15.1 multiply_reduce_fusion.16
  903.9 1.5 multiply_add_fusion.4
  906.3 4.8 convolution_convert_fusion.4
  911.1 2.0 copy.128
  913.1 2.0 fusion.89
  918.7 20.9 fusion.85
  941.2 9.0 fusion.93
  950.2 3.4 multiply_reduce_fusion.17
  956.4 20.1 add.321
  976.5 10.3 fusion.102
  986.8 5.1 fusion.97
  991.9 12.3 add.322
  1004.2 49.0 %add.324 = f32[1536,8192]{1,0:T(8,128)} add(f32[1536,8192]{1,0:T(8,128)} %get-tuple-element.772, f32[1536,8192]{1,0:T(8,128)} %fusion.85) | non-fusion elementwise | flops 12582912 | bytes 150994944 | tf_op jit(solution)/shard_map/cond/branch_1_fun/add | solution.py:162
  1053.3 26.0 add.325
  1080.5 124.3 %conditional.7 = (f32[128,1536]{1,0:T(8,128)}, f32[1536]{0:T(1024)S(1)}, f32[1536,3072]{1,0:T(8,128)}, f32[1536,1536]{1,0:T(8,128)}, f32[1536]{0:T(1024)S(1)}, /...) conditional(s32[]{:T(128)} %convert_element_type.309, (f32[1536]{0:T(1024)S(1)}, f32[1536,3072]{1,0:T(8,128)}, ...), branch_computations={%region_32.33_spmd, %region_33.40_spmd} | conditional | flops 13598703616 | bytes 380677440 | solution.py:281
  1081.9 12.9 multiply_convert_fusion.7
  1094.8 14.9 multiply_reduce_fusion.8
  1109.7 1.9 multiply_add_fusion.2
  1111.6 4.8 convolution_convert_fusion.2
  1116.5 1.9 copy.114
  1118.4 1.5 select_n.325
  1120.0 1.6 fusion.47
  1124.2 1.7 convolution_multiply_fusion.4
  1126.3 3.4 multiply_reduce_fusion.9
  1130.8 13.1 convolution_add_fusion.4
  1146.1 8.8 convolution_add_fusion.5
  1154.9 32.9 %convolution_add_fusion.2 = f32[1536,8192]{1,0:T(8,128)} fusion(f32[1536,8192]{1,0:T(8,128)} %get-tuple-element.690, bf16[128,4096]{1,0:T(8,128)(2,1)} %get-tuple-element.1262, bf16[128,4096]{1,0:T(8,128)(2,1)} %get-tuple-element.1261, bf16[128,1536]{1,0:T(8,128)(2,1)S(1)} %copy-done.51, bf16[128,1536]{1,0:T(8,128)(2,1)S(1)} %copy-done.20, ...), kind=kOutput, calls=%fused_computation.115 | convolution fusion | flops 3238199296 | bytes 103546880 | tf_op jit(solution)/shard_map/cond/branch_1_fun/dot_general | solution.py:23
  1187.8 16.7 convolution_add_fusion.3
  1215.1 113.1 %reduce-scatter.19.cloned.1.call-done = f32[96,1]{1,0:T(8,128)} async-done(((f32[1536,1]{1,0:T(8,128)}), f32[96,1]{1,0:T(8,128)}) %reduce-scatter.19.cloned.1.call-update) | async-done | bytes 400
  1329.6 126.2 %reduce-scatter.21.cloned.1.call-done = f32[96,1]{1,0:T(8,128)} async-done(((f32[1536,1]{1,0:T(8,128)}), f32[96,1]{1,0:T(8,128)}) %reduce-scatter.21.cloned.1.call-update) | async-done | bytes 400
  1457.2 175.1 %reduce-scatter.13.cloned.1.call-done = f32[1,96,1536]{2,1,0:T(8,128)} async-done(((f32[1,1536,1536]{2,1,0:T(8,128)}), f32[1,96,1536]{2,1,0:T(8,128)}) %reduce-scatter.13.cloned.1.call-update) | async-done | bytes 589840 | tf_op jit(solution)/shard_map/reduce_scatter | solution.py:294
  1632.3 290.7 %reduce-scatter.11.cloned.1.call-done = f32[1,96,3072]{2,1,0:T(8,128)} async-done(((f32[1,1536,3072]{2,1,0:T(8,128)}), f32[1,96,3072]{2,1,0:T(8,128)}) %reduce-scatter.11.cloned.1.call-update) | async-done | bytes 1179664 | tf_op jit(solution)/shard_map/reduce_scatter | solution.py:293
  1923.0 364.1 %reduce-scatter.17.cloned.1.call-done = f32[1,256,1536]{2,1,0:T(8,128)} async-done(((f32[1,4096,1536]{2,1,0:T(8,128)}), f32[1,256,1536]{2,1,0:T(8,128)}) %reduce-scatter.17.cloned.1.call-update) | async-done | bytes 1572880 | tf_op jit(solution)/shard_map/reduce_scatter | solution.py:297
  2287.1 700.0 %reduce-scatter.15.cloned.1.call-done = f32[1,96,8192]{2,1,0:T(8,128)} async-done(((f32[1,1536,8192]{2,1,0:T(8,128)}), f32[1,96,8192]{2,1,0:T(8,128)}) %reduce-scatter.15.cloned.1.call-update) | async-done | bytes 3145744 | tf_op jit(solution)/shard_map/reduce_scatter | solution.py:296
  (399 shorter events, 70.6 us)
Async XLA Ops:
  7.2 49.0 %copy-start.106 = (s32[2,128]{1,0:T(2,128)S(1)}, s32[2,128]{1,0:T(2,128)}, u32[]{:S(2)}) copy-start(s32[2,128]{1,0:T(2,128)} %param.19) | copy-start | bytes 3076
  7.2 633.4 %copy-start.67 = (bf16[2,128,1536]{2,1,0:T(8,128)(2,1)S(1)}, bf16[2,128,1536]{2,1,0:T(8,128)(2,1)}, u32[]{:S(2)}) copy-start(bf16[2,128,1536]{2,1,0:T(8,128)(2,1)} %param.17) | copy-start | bytes 2359300
  7.2 86.4 %all-gather.7.cloned.1.call-start = ((), (), s32[]{:S(2)}) async-start(), calls=%async_computation.7 | async-start | bytes 5013504 | tf_op jit(solution)/shard_map/all_gather | solution.py:218
  8.0 208.9 %all-gather.5.cloned.1.call-start = ((), (), s32[]{:S(2)}) async-start(), calls=%async_computation.6 | async-start | bytes 10027008 | tf_op jit(solution)/shard_map/all_gather | solution.py:217
  8.7 360.6 %all-gather.11.cloned.1.call-start = ((), (), s32[]{:S(2)}) async-start(), calls=%async_computation.9 | async-start | bytes 13369344 | tf_op jit(solution)/shard_map/all_gather | solution.py:221
  9.4 631.2 %all-gather.9.cloned.1.call-start = ((), (), s32[]{:S(2)}) async-start(), calls=%async_computation.8 | async-start | bytes 26738688 | tf_op jit(solution)/shard_map/all_gather | solution.py:220
  10.0 1318.2 %reduce-scatter.19.cloned.1.call-start = ((), (), s32[]{:S(2)}) async-start(), calls=%async_computation.14 | async-start | bytes 835584
  56.2 678.0 %copy-start.88 = (bf16[1536]{0:T(1024)(128)(2,1)}, bf16[1536]{0:T(1024)(128)(2,1)S(1)}, u32[]{:S(2)}) copy-start(bf16[1536]{0:T(1024)(128)(2,1)S(1)} %get-tuple-element.1215) | copy-start | bytes 9220
  56.2 678.0 %copy-start.90 = (bf16[1536]{0:T(1024)(128)(2,1)}, bf16[1536]{0:T(1024)(128)(2,1)S(1)}, u32[]{:S(2)}) copy-start(bf16[1536]{0:T(1024)(128)(2,1)S(1)} %get-tuple-element.1216) | copy-start | bytes 9220
  56.2 678.0 %copy-start.103 = (s32[128]{0:T(128)}, s32[128]{0:T(128)S(1)}, u32[]{:S(2)}) copy-start(s32[128]{0:T(128)S(1)} %broadcast_select_fusion.1) | copy-start | bytes 1540
  640.8 16.0 copy-start.10
  661.0 14.4 slice-start.12
  662.5 12.9 slice-start.13
  662.5 12.9 slice-start.14
  680.7 2.8 collective-permute-start
  682.4 17.8 copy-start.94
  683.2 12.1 copy-start.83
  685.5 11.2 copy-start.21
  685.7 48.5 %copy-start.109 = (f32[128,1]{0,1:T(1,128)}, f32[128,1]{0,1:T(1,128)S(1)}, u32[]{:S(2)}) copy-start(f32[128,1]{0,1:T(1,128)S(1)} %get-tuple-element.1313) | copy-start | bytes 1540
  700.1 10.4 copy-start.107
  700.1 34.1 %copy-start.111 = (f32[128,1]{0,1:T(1,128)}, f32[128,1]{0,1:T(1,128)S(1)}, u32[]{:S(2)}) copy-start(f32[128,1]{0,1:T(1,128)S(1)} %get-tuple-element.1311) | copy-start | bytes 1540
  700.2 13.7 slice-start.9
  700.3 13.5 slice-start.10
  700.3 13.5 slice-start.11
  715.7 4.6 collective-permute-start.1
  782.3 106.4 %copy-start.28 = (f32[128,1536]{1,0:T(8,128)}, f32[128,1536]{1,0:T(8,128)S(1)}, u32[]{:S(2)}) copy-start(f32[128,1536]{1,0:T(8,128)S(1)} %get-tuple-element.768) | copy-start | bytes 2359300
  782.4 94.8 %copy-start.37 = (bf16[2,128,1536]{2,1,0:T(8,128)(2,1)S(1)}, bf16[2,128,1536]{2,1,0:T(8,128)(2,1)}, u32[]{:S(2)}) copy-start(bf16[2,128,1536]{2,1,0:T(8,128)(2,1)} %param.18) | copy-start | bytes 2359300
  782.4 94.8 %collective-permute-start.2 = (bf16[128,1536]{1,0:T(8,128)(2,1)S(1)}, bf16[128,1536]{1,0:T(8,128)(2,1)S(1)}, u32[]{:S(2)}, u32[]{:S(2)}) collective-permute-start(bf16[128,1536]{1,0:T(8,128)(2,1)S(1)} %convert_element_type.327), channel_id=1, source_target_pairs={{16,0},{17,1},{18,2},{19,3},{20,4},{21,5},{22,6},{23,7},{24,8},{25... | collective-permute-start | bytes 1179656 | tf_op jit(solution)/shard_map/ppermute | solution.py:19
  785.9 102.9 %copy-start.95 = (f32[1536]{0:T(1024)S(1)}, f32[1536]{0:T(1024)}, u32[]{:S(2)}) copy-start(f32[1536]{0:T(1024)} %copy-done.94) | copy-start | bytes 18436
  785.9 102.9 %copy-start.108 = (f32[128]{0:T(128)S(1)}, f32[128]{0:T(128)}, u32[]{:S(2)}) copy-start(f32[128]{0:T(128)} %copy-done.107) | copy-start | bytes 1540
  877.2 11.6 copy-start.71
  918.7 20.9 copy-start.84
  918.7 20.9 copy-start.87
  939.6 10.5 slice-start
  955.0 124.2 %collective-permute-start.3 = (bf16[128,1536]{1,0:T(8,128)(2,1)}, bf16[128,1536]{1,0:T(8,128)(2,1)}, u32[]{:S(2)}, u32[]{:S(2)}) collective-permute-start(bf16[128,1536]{1,0:T(8,128)(2,1)} %get-tuple-element.1229), channel_id=1, source_target_pairs={{16,0},{17,1},{18,2},{19,3},{20,4},{21,5},{22,6},{23,7},{24,8},{25... | collective-permute-start | bytes 1179656 | tf_op jit(solution)/shard_map/ppermute | solution.py:19
  956.3 20.2 copy-start.38
  956.3 20.2 copy-start.72
  976.5 10.3 copy-start.15
  1053.2 27.2 copy-start.23
  1053.2 27.2 copy-start.46
  1053.2 27.2 copy-start.89
  1053.2 27.2 copy-start.91
  1053.2 27.2 copy-start.97
  1053.2 27.2 copy-start.101
  1053.2 27.2 copy-start.104
  1053.2 27.2 copy-start.105
  1053.3 27.2 copy-start.110
  1053.3 27.2 copy-start.112
  1053.3 27.2 copy-start.114
  1053.3 27.2 copy-start.121
  1053.3 27.2 copy-start.123
  1080.7 14.1 copy-start.19
  1080.7 14.1 copy-start.48
  1081.9 13.0 copy-start.68
  1094.8 14.9 copy-start.25
  1111.6 14.4 slice-start.6
  1130.8 14.3 copy-start.16
  1154.9 32.9 %copy-start.49 = (pred[128,4096]{1,0:T(32,128)(4,1)S(1)}, pred[128,4096]{1,0:T(32,128)(4,1)}, u32[]{:S(2)}) copy-start(pred[128,4096]{1,0:T(32,128)(4,1)} %copy-done.48) | copy-start | bytes 1572868 | tf_op jit(solution)/shard_map/cond
  1154.9 32.9 %copy-start.69 = (bf16[128,1536]{1,0:T(8,128)(2,1)S(1)}, bf16[128,1536]{1,0:T(8,128)(2,1)}, u32[]{:S(2)}) copy-start(bf16[128,1536]{1,0:T(8,128)(2,1)} %copy-done.68) | copy-start | bytes 1179652 | tf_op jit(solution)/shard_map/cond
  1206.0 249.8 %reduce-scatter.21.cloned.1.call-start = ((), (), s32[]{:S(2)}) async-start(), calls=%async_computation.15 | async-start | bytes 835584
  1207.2 425.1 %reduce-scatter.13.cloned.1.call-start = ((), (), s32[]{:S(2)}) async-start(), calls=%async_computation.11 | async-start | bytes 10027008 | tf_op jit(solution)/shard_map/reduce_scatter | solution.py:294
  1208.0 715.1 %reduce-scatter.11.cloned.1.call-start = ((), (), s32[]{:S(2)}) async-start(), calls=%async_computation.10 | async-start | bytes 20054016 | tf_op jit(solution)/shard_map/reduce_scatter | solution.py:293
  1208.7 1078.4 %reduce-scatter.17.cloned.1.call-start = ((), (), s32[]{:S(2)}) async-start(), calls=%async_computation.13 | async-start | bytes 26738688 | tf_op jit(solution)/shard_map/reduce_scatter | solution.py:297
  1209.4 1777.7 %reduce-scatter.15.cloned.1.call-start = ((), (), s32[]{:S(2)}) async-start(), calls=%async_computation.12 | async-start | bytes 53477376 | tf_op jit(solution)/shard_map/reduce_scatter | solution.py:296
  (69 other events, 256.1 us)
Sparse Core Ops, SparseCore 0:
  10.8 82.7 all-gather.6
  96.4 120.3 all-gather.4
  219.7 149.5 all-gather.10
  371.9 268.6 all-gather.8
  1206.1 122.0 reduce-scatter.18
  1332.8 122.9 reduce-scatter.20
  1462.1 170.2 reduce-scatter.12
  1638.7 284.2 reduce-scatter.10
  1929.3 357.7 reduce-scatter.16
  2293.5 693.5 reduce-scatter.14
where the time goes:
time: 3000 us; the launch traced here: 2990 us
  waiting for transfers between devices  2450 us (82%)
  matrix products  245 us (8%)
  other arithmetic  143 us (5%)
  local copies, waits for them, and re-layouts  80.7 us (3%)
  blocking collectives  44.4 us (1%)
    reduce_scatter x1, waiting for transfers between devices, shards(): lax.psum_scatter(totals[4][None], 'dp', scatter_dimension=1, tiled=True)  700 us
    reduce_scatter x1, waiting for transfers between devices, shards(): lax.psum_scatter(totals[5][None], 'dp', scatter_dimension=1, tiled=True)  364 us
    reduce_scatter x1, waiting for transfers between devices, shards(): lax.psum_scatter(totals[1][None], 'dp', scatter_dimension=1, tiled=True)  291 us
    all_gather x1, waiting for transfers between devices, shards(): lax.all_gather(w_gate_up, 'dp', axis=1, tiled=True)  271 us
    unnamed x12, waiting for transfers between devices  245 us
    reduce_scatter x1, waiting for transfers between devices, shards(): lax.psum_scatter(totals[2][None], 'dp', scatter_dimension=1, tiled=True)  175 us
    all_gather x1, waiting for transfers between devices, shards(): lax.all_gather(w_down, 'dp', axis=1, tiled=True)  152 us
    all_gather x1, waiting for transfers between devices, shards(): lax.all_gather(w_qkv, 'dp', axis=1, tiled=True)  123 us
  transfers between devices with their start and end apart: 14, of which 12 were waited for; matrix products, arithmetic and copies ran while one was open for 5% of the time, Pallas kernels for 0%

commit v1 on v0

v1 whole, which is shorter than its diff:
```python
import jax
import jax.numpy as jnp
from jax import lax
from jax.sharding import Mesh, PartitionSpec as P

D = 1536
HEADS = 16
KV_HEADS = 8
HEAD_WIDTH = 96
FF = 4096

rms_eps = 1e-05
rope_base = 10000.0

AXES = ("section", "h", "g", "y", "x", "w")
DP = ("h", "g", "y", "x", "w")
bf16 = jnp.bfloat16
f32 = jnp.float32


def swap(value, axis):
    return lax.ppermute(value, axis, [(0, 1), (1, 0)])


def dot(a, b):
    return lax.dot_general(a, b, (((1,), (0,)), ((), ())), preferred_element_type=f32)


def dot_tn(a, b):
    return lax.dot_general(a, b, (((0,), (0,)), ((), ())), preferred_element_type=f32)


def dot_nt(a, b):
    return lax.dot_general(a, b, (((1,), (1,)), ((), ())), preferred_element_type=f32)


def to_order(value, rest):
    lead = value.shape[:-1]
    n = len(lead)
    split = value.reshape(lead + (2, 2, 2, 2, rest, -1))
    order = tuple(range(n)) + (n + 3, n + 4, n + 2, n, n + 1, n + 5)
    return split.transpose(order).reshape(value.shape)


def from_order(value, rest):
    lead = value.shape[:-1]
    n = len(lead)
    split = value.reshape(lead + (2, rest, 2, 2, 2, -1))
    order = tuple(range(n)) + (n + 3, n + 4, n + 2, n, n + 1, n + 5)
    return split.transpose(order).reshape(value.shape)


def by_bit(bit, mine, theirs, axis):
    first = jnp.where(bit == 0, mine, theirs)
    last = jnp.where(bit == 0, theirs, mine)
    return jnp.stack([first, last], axis=axis)


def pick(bit, value, axis):
    return lax.dynamic_index_in_dim(value, bit, axis, keepdims=False)


def relative(bit, value):
    half = value.shape[-1] // 2
    turned = jnp.concatenate([value[..., half:], value[..., :half]], axis=-1)
    return jnp.where(bit == 0, value, turned)


def gather2(value):
    return jnp.concatenate([value, swap(value, "g")], axis=0)


def scatter2(part):
    rows = part.shape[0] // 2
    return part[:rows] + swap(part[rows:].astype(bf16), "g").astype(f32)


def gather4(value):
    half = value.shape[0] // 2
    across_y = swap(value, "y")
    across_g = swap(value, "g")
    corner_a = swap(across_y[:half], "g")
    corner_b = swap(across_g[half:], "y")
    return jnp.concatenate([value, across_y, across_g, corner_a, corner_b], axis=0)


def scatter4(part):
    rows = part.shape[0] // 4
    half = rows // 2
    own, for_y, for_g, corner = (part[i * rows : (i + 1) * rows] for i in range(4))
    low = corner.astype(bf16)
    from_g = swap(low[:half], "g").astype(f32)
    from_y = swap(low[half:], "y").astype(f32)
    send_y = jnp.concatenate([for_y[:half] + from_g, for_y[half:]], axis=0).astype(bf16)
    send_g = jnp.concatenate([for_g[:half], for_g[half:] + from_y], axis=0).astype(bf16)
    return own + (swap(send_y, "y").astype(f32) + swap(send_g, "g").astype(f32))


def rms_scale(value):
    return lax.rsqrt(jnp.mean(value * value, axis=-1, keepdims=True) + rms_eps)


def norm_back(value, scale_rows, gain_row, incoming):
    unit_rows = value * scale_rows
    grad_gain = jnp.sum(incoming * unit_rows, axis=0)
    grad_unit = incoming * gain_row
    grad_value = scale_rows * (
        grad_unit - unit_rows * jnp.mean(grad_unit * unit_rows, axis=-1, keepdims=True)
    )
    return grad_value, grad_gain


def rotary(labels):
    length = labels.shape[-1]
    same_doc = labels[:, :, None] == labels[:, None, :]
    indices = jnp.arange(length)
    before = indices[None, :] < indices[:, None]
    places = jnp.sum(jnp.where(same_doc & before[None], 1, 0), axis=2).astype(f32)
    half_dim = HEAD_WIDTH // 2
    frequency = rope_base ** (-jnp.arange(half_dim, dtype=f32) / half_dim)
    angles = places[:, :, None] * frequency
    allowed = same_doc & (indices[None, :] <= indices[:, None])[None]
    return jnp.cos(angles), jnp.sin(angles), allowed


def rotate(heads, cos_table, sin_table):
    half_dim = HEAD_WIDTH // 2
    front = heads[..., :half_dim]
    back = heads[..., half_dim:]
    cosine = cos_table[:, :, None, :]
    sine = sin_table[:, :, None, :]
    return jnp.concatenate([front * cosine - back * sine, back * cosine + front * sine], axis=-1)


def split_heads(joined, seqs, length):
    q = joined[:, :384].reshape(seqs, length, 4, HEAD_WIDTH)
    k = joined[:, 384:576].reshape(seqs, length, 2, HEAD_WIDTH)
    v = joined[:, 576:].reshape(seqs, length, 2, HEAD_WIDTH)
    return q, k, v


def attention(joined, tables, seqs, length):
    cos_table, sin_table, allowed = tables
    q, k, v = split_heads(joined, seqs, length)
    q = rotate(q, cos_table, sin_table).astype(bf16).reshape(seqs, length, 2, 2, HEAD_WIDTH)
    k = rotate(k, cos_table, sin_table).astype(bf16)
    v = v.astype(bf16)
    scores = jnp.einsum("btxyd,buyd->bxytu", q, k, preferred_element_type=f32) * HEAD_WIDTH ** (-0.5)
    scores = jnp.where(allowed[:, None, None], scores, -1e30)
    peak = jnp.max(scores, axis=-1, keepdims=True)
    lse = peak + jnp.log(jnp.sum(jnp.exp(scores - peak), axis=-1, keepdims=True))
    probs = jnp.exp(scores - lse)
    mixed = jnp.einsum("bxytu,buyd->btxyd", probs.astype(bf16), v, preferred_element_type=f32)
    mixed = mixed.astype(bf16).reshape(seqs * length, 4 * HEAD_WIDTH)
    return mixed, (q, k, v, probs)


def attention_back(go, kept, tables, seqs, length):
    cos_table, sin_table, _ = tables
    q, k, v, probs = kept
    go = go.astype(bf16).reshape(seqs, length, 2, 2, HEAD_WIDTH)
    grad_v = jnp.einsum("bxytu,btxyd->buyd", probs.astype(bf16), go, preferred_element_type=f32)
    dp = jnp.einsum("btxyd,buyd->bxytu", go, v, preferred_element_type=f32)
    row = jnp.sum(dp * probs, axis=-1, keepdims=True)
    dsc = (probs * (dp - row)).astype(bf16)
    scale = HEAD_WIDTH ** (-0.5)
    grad_q = jnp.einsum("bxytu,buyd->btxyd", dsc, k, preferred_element_type=f32) * scale
    grad_k = jnp.einsum("bxytu,btxyd->buyd", dsc, q, preferred_element_type=f32) * scale
    rows = seqs * length
    grad_q = rotate(grad_q.reshape(seqs, length, 4, HEAD_WIDTH), cos_table, -sin_table)
    grad_k = rotate(grad_k, cos_table, -sin_table)
    return jnp.concatenate(
        [grad_q.reshape(rows, 384), grad_k.reshape(rows, 192), grad_v.reshape(rows, 192)], axis=1
    ).astype(bf16)


def shards(tokens, cotangent, segments, gain_attn, w_qkv, w_out, gain_mlp, w_gate_up, w_down):
    core = lax.axis_index("section")
    hb = lax.axis_index("h")
    xb = lax.axis_index("x")
    rest = lax.axis_size("w")
    length = tokens.shape[1]
    rows = w_qkv.shape[1]
    units = w_down.shape[1] // 2
    place = lax.axis_index(DP)

    def all_reduce(value):
        for axis in ("section", "g", "y", "x", "h"):
            value = value + swap(value, axis)
        return lax.psum(value, "w") if rest > 1 else value

    def over_w(value):
        return lax.all_gather(value, "w", axis=0) if rest > 1 else value[None]

    gains = jnp.zeros((2, 2, D), f32)
    own_gains = jnp.stack([gain_attn[0], gain_mlp[0]]).astype(f32)
    gains = lax.dynamic_update_slice(gains, own_gains[None], (core, 0, place * rows))
    gains = to_order(all_reduce(gains), rest)

    def quarter(part, order):
        return part.transpose(order)

    q = w_qkv[0, :, :D].reshape(rows, 2, 2, 2, 2, HEAD_WIDTH).transpose(1, 2, 0, 4, 3, 5)
    k = w_qkv[0, :, D : D + D // 2].reshape(rows, 2, 2, 192).transpose(1, 2, 0, 3)
    v = w_qkv[0, :, D + D // 2 :].reshape(rows, 2, 2, 192).transpose(1, 2, 0, 3)
    qkv = jnp.concatenate([q.reshape(4, rows, 384), k.reshape(4, rows, 192), v.reshape(4, rows, 192)], axis=2)
    qkv = lax.all_to_all(qkv, ("section", "g"), 0, 0, tiled=True).reshape(2, 2, rows, 768)

    out = lax.all_gather(to_order(w_out[0], rest), "section", axis=0)
    out = jnp.where(hb == core, out, swap(out, "h"))

    up = w_gate_up[0].reshape(rows, 2, 2, 2, 2, 2, rest, 2, units)
    up = up.transpose(7, 4, 3, 0, 1, 5, 6, 2, 8)
    slice_width = 2 * 2 * rest * 2 * units
    up = up.reshape(8, rows, slice_width)
    up = lax.all_to_all(up, ("section", "y", "g"), 0, 0, tiled=True).reshape(2, 2, 2, rows, slice_width)

    down = to_order(w_down[0], rest).reshape(2, units, D)
    down = lax.all_to_all(down, "section", 0, 0, tiled=True)

    def attn_weights(layer):
        part = by_bit(hb, qkv[layer], swap(qkv[layer], "h"), 0).reshape(4 * rows, 768)
        wide = lax.all_gather(part, ("x", "w", "y"), axis=0, tiled=True)
        tall = lax.all_gather(out[layer], ("x", "y", "w"), axis=0, tiled=True)
        return (wide, swap(wide, "section")), (tall, swap(tall, "section"))

    def mlp_weights(layer):
        part = by_bit(hb, up[layer], swap(up[layer], "h"), 1)
        part = over_w(part).reshape(D // 2, slice_width)
        other = swap(part, "x")
        tall = over_w(by_bit(hb, down[layer], swap(down[layer], "h"), 0)).reshape(rest * 2 * units, D)
        tall_other = swap(tall, "x")
        wide = ((part, other), (swap(part, "section"), swap(other, "section")))
        high = ((tall, tall_other), (swap(tall, "section"), swap(tall_other, "section")))
        return wide, high

    own = lax.dynamic_index_in_dim(segments, core, 0, keepdims=True)
    labels = gather2(own)
    tables = rotary(labels)

    def forward(hidden, attn, mlp, gain):
        (wide_m, wide_t), (tall_m, tall_t) = attn
        scale_one = rms_scale(hidden)
        normed = gather2((hidden * scale_one * gain[0]).astype(bf16))
        mixed_m, kept_m = attention(dot(normed, wide_m), tables, 2, length)
        mixed_t, kept_t = attention(dot(normed, wide_t), tables, 2, length)
        middle = hidden + scatter2(dot(mixed_m, tall_m) + dot(mixed_t, tall_t))
        scale_two = rms_scale(middle)
        second = (middle * scale_two * gain[1]).astype(bf16)
        second = gather4(relative(xb, second))
        halves = (second[:, : D // 2], second[:, D // 2 :])
        parts = []
        total = 0.0
        for (near, far), (tall, tall_other) in zip(*mlp):
            gate_up = dot(halves[0], near) + dot(halves[1], far)
            gate = gate_up[:, : slice_width // 2]
            lift = gate_up[:, slice_width // 2 :]
            inner = relative(xb, (jax.nn.silu(gate) * lift).astype(bf16))
            mid = inner.shape[1] // 2
            total = total + dot(inner[:, :mid], tall) + dot(inner[:, mid:], tall_other)
            parts.append((gate, lift, inner))
        result = middle + scatter4(total)
        kept = (hidden, scale_one, normed, (mixed_m, mixed_t), (kept_m, kept_t), middle, scale_two, halves, parts)
        return result, kept

    def combine(mine, theirs):
        return (mine + swap(theirs.astype(bf16), "section").astype(f32)).astype(bf16)

    def over_h(value, axis):
        mine = pick(hb, value, axis)
        return mine.astype(f32) + swap(pick(1 - hb, value, axis), "h").astype(f32)

    def scatter_w(value):
        if rest == 1:
            return value
        return lax.psum_scatter(value, "w", scatter_dimension=0, tiled=True)

    def backward(grad, kept, attn, mlp, gain):
        (wide_m, wide_t), (tall_m, tall_t) = attn
        hidden, scale_one, normed, mixed, kept_attn, middle, scale_two, halves, parts = kept
        low = gather4(grad.astype(bf16))
        grad_near = 0.0
        grad_far = 0.0
        pieces = []
        for ((near, far), (tall, tall_other)), (gate, lift, inner) in zip(zip(*mlp), parts):
            mid = inner.shape[1] // 2
            down_near = dot_tn(inner[:, :mid], low)
            down_far = dot_tn(inner[:, mid:], low)
            gi = jnp.concatenate([dot_nt(low, tall), dot_nt(low, tall_other)], axis=1)
            gi = relative(xb, gi)
            sig = jax.nn.sigmoid(gate)
            g_gate = gi * lift * sig * (1.0 + gate * (1.0 - sig))
            g_up = gi * gate * sig
            gg = jnp.concatenate([g_gate, g_up], axis=1).astype(bf16)
            pieces.append((down_near, down_far, dot_tn(halves[0], gg), dot_tn(halves[1], gg)))
            grad_near = grad_near + dot_nt(gg, near)
            grad_far = grad_far + dot_nt(gg, far)
        gs = relative(xb, scatter4(jnp.concatenate([grad_near, grad_far], axis=1)))

        down_near, down_far, up_near, up_far = (combine(a, b) for a, b in zip(*pieces))
        grad_down = down_near.astype(f32) + swap(down_far, "x").astype(f32)
        grad_up = up_near.astype(f32) + swap(up_far, "x").astype(f32)
        grad_down = scatter_w(grad_down.astype(bf16)).reshape(2, units, D)
        grad_down = over_h(grad_down, 0).astype(bf16)
        grad_up = scatter_w(grad_up.astype(bf16)).reshape(2, 2, 2, rows, slice_width)
        grad_up = over_h(grad_up, 1).astype(bf16)

        gm, gain_two = norm_back(middle, scale_two, gain[1], gs)
        gm = gm + grad
        gmb = gather2(gm.astype(bf16))
        grad_out = combine(dot_tn(mixed[0], gmb), dot_tn(mixed[1], gmb))
        grad_out = lax.psum_scatter(grad_out, ("x", "y", "w"), scatter_dimension=0, tiled=True)
        grad_out = (grad_out.astype(f32) + swap(grad_out, "h").astype(f32)).astype(bf16)
        gq_m = attention_back(dot_nt(gmb, tall_m), kept_attn[0], tables, 2, length)
        gq_t = attention_back(dot_nt(gmb, tall_t), kept_attn[1], tables, 2, length)
        gn = scatter2(dot_nt(gq_m, wide_m) + dot_nt(gq_t, wide_t))
        grad_qkv = combine(dot_tn(normed, gq_m), dot_tn(normed, gq_t))
        grad_qkv = lax.psum_scatter(grad_qkv, ("x", "w", "y"), scatter_dimension=0, tiled=True)
        grad_qkv = over_h(grad_qkv.reshape(2, 2, rows, 768), 0).astype(bf16)
        grad_in, gain_one = norm_back(hidden, scale_one, gain[0], gn)
        return grad_in + gm, (grad_qkv, grad_out, grad_up, grad_down, jnp.stack([gain_one, gain_two]))

    start = to_order(pick(core, tokens, 0).astype(f32), rest)
    attn = [attn_weights(0), None]
    mlp = [mlp_weights(0), None]
    attn[1] = attn_weights(1)
    mlp[1] = mlp_weights(1)
    first, kept_first = forward(start, attn[0], mlp[0], gains[0])
    handed = first.astype(bf16)
    last, kept_last = forward(handed.astype(f32), attn[1], mlp[1], gains[1])
    acts = from_order(jnp.stack([handed, last.astype(bf16)]), rest)
    acts = lax.all_to_all(acts, "section", 0, 0, tiled=True)[None]

    grad = to_order(pick(core, cotangent, 0).astype(f32), rest)
    grad_last, grads_last = backward(grad, kept_last, attn[1], mlp[1], gains[1])
    handed_back = grad_last.astype(bf16).astype(f32)
    grad_first, grads_first = backward(handed_back, kept_first, attn[0], mlp[0], gains[0])
    input_grads = from_order(jnp.stack([grad_first, grad_last]), rest)
    input_grads = lax.all_to_all(input_grads, "section", 0, 0, tiled=True)[None]

    both = [jnp.stack(pair) for pair in zip(grads_first, grads_last)]
    grad_qkv = lax.all_to_all(both[0].reshape(4, rows, 768), ("section", "g"), 0, 0, tiled=True)
    gq = grad_qkv[:, :, :384].reshape(2, 2, rows, 2, 2, HEAD_WIDTH).transpose(2, 0, 1, 4, 3, 5)
    gk = grad_qkv[:, :, 384:576].transpose(1, 0, 2)
    gv = grad_qkv[:, :, 576:].transpose(1, 0, 2)
    grad_qkv = jnp.concatenate([part.reshape(rows, -1) for part in (gq, gk, gv)], axis=1).astype(f32)[None]

    mine = pick(core, both[1], 0)
    grad_out = jnp.where(hb == core, mine, swap(pick(1 - core, both[1], 0), "section"))
    grad_out = from_order(grad_out.astype(f32), rest)[None]

    grad_up = lax.all_to_all(both[2].reshape(8, rows, slice_width), ("section", "y", "g"), 0, 0, tiled=True)
    grad_up = grad_up.reshape(2, 2, 2, rows, 2, 2, rest, 2, units).transpose(3, 4, 7, 2, 1, 5, 6, 0, 8)
    grad_up = grad_up.reshape(rows, 2 * FF).astype(f32)[None]

    grad_down = lax.all_to_all(both[3], "section", 0, 0, tiled=True).reshape(2 * units, D)
    grad_down = from_order(grad_down.astype(f32), rest)[None]

    gain_sums = from_order(all_reduce(both[4]), rest)
    gain_sums = lax.dynamic_slice(gain_sums, (core, 0, place * rows), (1, 2, rows))
    return (
        acts,
        input_grads,
        gain_sums[:, 0],
        grad_qkv,
        grad_out,
        gain_sums[:, 1],
        grad_up,
        grad_down,
    )


def solution(mesh):
    count = mesh.shape["dp"]
    wide = Mesh(mesh.devices.reshape(2, 2, 2, 2, 2, count // 16), AXES)
    in_specs = (
        P(DP, None, None),
        P(DP, None, None),
        P(DP, None),
        P("section", DP),
        P("section", DP, None),
        P("section", DP, None),
        P("section", DP),
        P("section", DP, None),
        P("section", DP, None),
    )
    out_specs = (
        P("section", DP, None, None),
        P("section", DP, None, None),
        P("section", DP),
        P("section", DP, None),
        P("section", DP, None),
        P("section", DP),
        P("section", DP, None),
        P("section", DP, None),
    )
    return jax.shard_map(shards, mesh=wide, in_specs=in_specs, out_specs=out_specs, check_vma=False)
```

time: 3000 us -> 940 us (0.31)
  waiting for transfers between devices: 2450 us -> 400 us
  starting transfers between devices: 7.67 us -> 124 us
  other arithmetic: 143 us -> 63.6 us
  matrix products: 245 us -> 167 us
  local copies, waits for them, and re-layouts: 80.7 us -> 129 us
    reduce_scatter x4, waiting for transfers between devices: 1530 us -> 0.05 us  [the longest x2 0.02 us: backward(): lax.psum_scatter(grad_out, ('x', 'y', 'w'), scatter_dimension=0, tiled=True)]
    all_gather x4, waiting for transfers between devices: 583 us -> 23.6 us  [the longest x2 23.6 us: attn_weights(): tall = lax.all_gather(out[layer], ('x', 'y', 'w'), axis=0, tiled=True)]
    ppermute x4 -> x99, waiting for transfers between devices: 91.7 us -> 376 us  [swap(): return lax.ppermute(value, axis, [(0, 1), (1, 0)])]
    unnamed x12 -> x8, waiting for transfers between devices: 245 us -> 0.13 us
    add x13 -> x16, other arithmetic: 112 us -> 4.07 us  [the longest x9 2.38 us: all_reduce(): value = value + swap(value, axis)]
    ppermute x4 -> x99, starting transfers between devices: 7.28 us -> 102 us  [swap(): return lax.ppermute(value, axis, [(0, 1), (1, 0)])]
    dot_general x37 -> x96, matrix products: 245 us -> 167 us  [the longest x24 63.4 us: dot_tn(): lax.dot_general(a, b, (((0,), (0,)), ((), ())), preferred_element_type=f32)]
    squeeze x1 -> x0, blocking collectives: 44.4 us -> none  [shards(): weights = tuple((shard_part[0] for shard_part in gathered))]
  transfers between devices with their start and end apart: 14 -> 112, of which waited for: 12 -> 43; matrix products, arithmetic and copies ran while one was open for 5% -> 34% of each run, Pallas kernels for 0% -> 0%
where the time goes in v1:
time: 940 us; the launch traced here: 930 us
  waiting for transfers between devices  400 us (43%)
  matrix products  167 us (18%)
  local copies, waits for them, and re-layouts  129 us (14%)
  starting transfers between devices  124 us (13%)
  other arithmetic  63.6 us (7%)
  blocking collectives  26.4 us (3%)
  between operations  18.7 us (2%)
    ppermute x99, waiting for transfers between devices, swap(): return lax.ppermute(value, axis, [(0, 1), (1, 0)])  376 us
    ppermute x99, starting transfers between devices, swap(): return lax.ppermute(value, axis, [(0, 1), (1, 0)])  102 us
    dot_general x24, matrix products, dot_tn(): lax.dot_general(a, b, (((0,), (0,)), ((), ())), preferred_element_type=f32)  63.4 us
    dot_general x24, matrix products, dot_nt(): lax.dot_general(a, b, (((1,), (1,)), ((), ())), preferred_element_type=f32)  47.5 us
    unnamed x490, local copies, waits for them, and re-layouts  44.4 us
    dot_general x24, matrix products, dot(): lax.dot_general(a, b, (((1,), (0,)), ((), ())), preferred_element_type=f32)  43.6 us
    all_gather x2, waiting for transfers between devices, attn_weights(): tall = lax.all_gather(out[layer], ('x', 'y', 'w'), axis=0, tiled=True)  23.6 us
  transfers between devices with their start and end apart: 112, of which 43 were waited for; matrix products, arithmetic and copies ran while one was open for 34% of the time, Pallas kernels for 0%

profile of v1, /device:TPU:0, one launch (start us, length us, event | category | flops | bytes accessed | tf_op | source)
XLA Modules:
  0.0 929.5 jit_solution(2342148365501639993)
XLA Ops:
  9.7 13.6 %all_to_all.40 = bf16[4,96,768]{2,1,0:T(8,128)(2,1)S(1)} all-to-all(bf16[4,96,768]{2,1,0:T(8,128)(2,1)S(1)} %pad_maximum_fusion.16), channel_id=1, replica_groups=mesh['section'=2,'h'=2,'g'=2,'y'=2,'x'=2,'w'=1] {'section','g'}, dimensions={0} | all-to-all | bytes 1179648 | tf_op jit(solution)/shard_map/all_to_all | solution.py:207
  26.1 13.3 %collective-permute-done.6 = bf16[2,96,768]{2,1,0:T(8,128)(2,1)S(1)} collective-permute-done((bf16[2,96,768]{2,1,0:T(8,128)(2,1)S(1)}, bf16[2,96,768]{2,1,0:T(8,128)(2,1)S(1)}, u32[]{:S(2)}, u32[]{:S(2)}) %collective-permute-start.6) | collective-permute-done | bytes 294944 | tf_op jit(solution)/shard_map/ppermute | solution.py:22
  47.1 3.0 collective-permute-start.8
  51.6 4.5 all-to-all-start.2
  60.8 3.6 all-to-all-start.1
  77.3 33.6 %collective-permute-done.1 = f32[2,2,1536]{2,1,0:T(2,128)S(1)} collective-permute-done((f32[2,2,1536]{2,1,0:T(2,128)}, f32[2,2,1536]{2,1,0:T(2,128)S(1)}, u32[]{:S(2)}, u32[]{:S(2)}) %collective-permute-start.1) | collective-permute-done | bytes 24608 | tf_op jit(solution)/shard_map/ppermute | solution.py:22
  121.2 3.4 collective-permute-done.4
  127.8 2.9 collective-permute-start.29
  130.7 11.4 %all-gather.11.cloned.1.call-done = bf16[1,384,1536]{2,1,0:T(8,128)(2,1)} async-done(((bf16[1,96,1536]{2,1,0:T(8,128)(2,1)}), bf16[1,384,1536]{2,1,0:T(8,128)(2,1)}) %all-gather.11.cloned.1.call-update) | async-done | bytes 1179664 | tf_op jit(solution)/shard_map/all_gather | solution.py:224
  165.7 15.9 %collective-permute-done.16 = bf16[2,2,96,1024]{3,2,1,0:T(8,128)(2,1)} collective-permute-done((bf16[2,2,96,1024]{3,2,1,0:T(8,128)(2,1)}, bf16[2,2,96,1024]{3,2,1,0:T(8,128)(2,1)}, u32[]{:S(2)}, u32[]{:S(2)}) %collective-permute-start.16) | collective-permute-done | bytes 786464 | tf_op jit(solution)/shard_map/ppermute | solution.py:22
  185.8 4.0 collective-permute-done.11
  192.9 28.6 %collective-permute-done.17 = bf16[768,1024]{1,0:T(8,128)(2,1)} collective-permute-done((bf16[768,1024]{1,0:T(8,128)(2,1)}, bf16[768,1024]{1,0:T(8,128)(2,1)}, u32[]{:S(2)}, u32[]{:S(2)}) %collective-permute-start.17) | collective-permute-done | bytes 1572896 | tf_op jit(solution)/shard_map/ppermute | solution.py:22
  226.8 6.5 collective-permute-done.13
  234.5 5.2 collective-permute-done.14
  241.9 3.6 collective-permute-done.15
  247.6 2.9 collective-permute-done.19
  256.4 2.8 fusion.87
  285.3 6.7 collective-permute-done.39
  294.4 2.7 concatenate.289
  297.1 12.2 %all-gather.13.cloned.1.call-done = bf16[1,384,1536]{2,1,0:T(8,128)(2,1)} async-done(((bf16[1,96,1536]{2,1,0:T(8,128)(2,1)}), bf16[1,384,1536]{2,1,0:T(8,128)(2,1)}) %all-gather.13.cloned.1.call-update) | async-done | bytes 1179664 | tf_op jit(solution)/shard_map/all_gather | solution.py:224
  313.3 33.8 %collective-permute-done.37 = bf16[2,2,96,1024]{3,2,1,0:T(8,128)(2,1)S(1)} collective-permute-done((bf16[2,2,96,1024]{3,2,1,0:T(8,128)(2,1)S(1)}, bf16[2,2,96,1024]{3,2,1,0:T(8,128)(2,1)S(1)}, u32[]{:S(2)}, u32[]{:S(2)}) %collective-permute-start.37) | collective-permute-done | bytes 786464 | tf_op jit(solution)/shard_map/ppermute | solution.py:22
  348.7 8.9 collective-permute-done.28
  385.2 7.8 collective-permute-done.38
  403.1 3.3 collective-permute-done.33
  416.3 2.7 fusion.81
  419.1 2.9 convolution_add_fusion.16
  461.7 10.1 %collective-permute-done.54 = bf16[128,1536]{1,0:T(8,128)(2,1)S(1)} collective-permute-done((bf16[128,1536]{1,0:T(8,128)(2,1)S(1)}, bf16[128,1536]{1,0:T(8,128)(2,1)S(1)}, u32[]{:S(2)}, u32[]{:S(2)}) %collective-permute-start.54) | collective-permute-done | bytes 393248 | tf_op jit(solution)/shard_map/ppermute | solution.py:22
  473.7 8.8 collective-permute-done.46
  488.7 4.3 all-to-all-start.3
  527.0 5.1 collective-permute-done.58
  537.5 4.5 add_convert_fusion.4
  543.8 3.6 add_convert_fusion.3
  554.4 5.0 collective-permute-done.60
  562.3 2.9 collective-permute-done.62
  577.8 2.8 fusion.197
  592.0 3.6 collective-permute-done.63
  595.6 3.0 collective-permute-start.98
  599.6 10.5 %collective-permute-done.98 = bf16[128,1536]{1,0:T(8,128)(2,1)S(1)} collective-permute-done((bf16[128,1536]{1,0:T(8,128)(2,1)S(1)}, bf16[128,1536]{1,0:T(8,128)(2,1)S(1)}, u32[]{:S(2)}, u32[]{:S(2)}) %collective-permute-start.98) | collective-permute-done | bytes 393248 | tf_op jit(solution)/shard_map/ppermute | solution.py:22
  611.7 7.1 collective-permute-done.66
  624.7 2.9 fusion.3
  630.6 4.0 collective-permute-done.67
  648.7 2.9 fusion.2
  660.2 3.9 add_convert_fusion
  665.7 3.4 convolution_convert_fusion.1
  671.6 2.9 convolution_add_fusion.8
  679.3 6.4 collective-permute-done.68
  691.8 3.5 collective-permute-start.90
  695.4 3.8 add_convert_fusion.6
  699.5 4.0 add_convert_fusion.1
  706.4 5.9 collective-permute-done.93
  714.4 4.4 collective-permute-start.94
  721.2 36.3 %collective-permute-done.85 = bf16[768,1024]{1,0:T(8,128)(2,1)} collective-permute-done((bf16[768,1024]{1,0:T(8,128)(2,1)}, bf16[768,1024]{1,0:T(8,128)(2,1)}, u32[]{:S(2)}, u32[]{:S(2)}) %collective-permute-start.85) | collective-permute-done | bytes 1572896 | tf_op jit(solution)/shard_map/ppermute | solution.py:22
  759.7 3.6 collective-permute-start.86
  765.8 30.5 %collective-permute-done.86 = bf16[2,2,96,1024]{3,2,1,0:T(8,128)(2,1)S(1)} collective-permute-done((bf16[2,2,96,1024]{3,2,1,0:T(8,128)(2,1)S(1)}, bf16[2,2,96,1024]{3,2,1,0:T(8,128)(2,1)S(1)}, u32[]{:S(2)}, u32[]{:S(2)}) %collective-permute-start.86) | collective-permute-done | bytes 786464 | tf_op jit(solution)/shard_map/ppermute | solution.py:22
  797.8 5.1 all_to_all.41
  802.9 5.2 all_to_all.42
  808.1 3.9 all-to-all-start.6
  817.0 21.9 %collective-permute-done.70 = f32[2,2,1536]{2,1,0:T(2,128)S(1)} collective-permute-done((f32[2,2,1536]{2,1,0:T(2,128)S(1)}, f32[2,2,1536]{2,1,0:T(2,128)S(1)}, u32[]{:S(2)}, u32[]{:S(2)}) %collective-permute-start.70) | collective-permute-done | bytes 24608 | tf_op jit(solution)/shard_map/ppermute | solution.py:22
  861.7 18.5 %collective-permute-done.79 = bf16[96,1536]{1,0:T(8,128)(2,1)S(1)} collective-permute-done((bf16[96,1536]{1,0:T(8,128)(2,1)}, bf16[96,1536]{1,0:T(8,128)(2,1)S(1)}, u32[]{:S(2)}, u32[]{:S(2)}) %collective-permute-start.79) | collective-permute-done | bytes 294944 | tf_op jit(solution)/shard_map/ppermute | solution.py:22
  880.2 6.3 collective-permute-done.77
  887.6 3.1 collective-permute-done.75
  891.7 4.2 all-to-all-start.5
  906.7 4.5 reshape.599
  913.6 3.8 copy.841
  (1076 shorter events, 404.6 us)
Async XLA Ops:
  7.2 110.2 %all-gather.7.cloned.1.call-start = ((), (), s32[]{:S(2)}) async-start(), calls=%async_computation.12 | async-start | bytes 2949120 | tf_op jit(solution)/shard_map/all_gather | solution.py:223
  43.0 31.5 %collective-permute-start = (f32[2,2,1536]{2,1,0:T(2,128)}, f32[2,2,1536]{2,1,0:T(2,128)}, u32[]{:S(2)}, u32[]{:S(2)}) collective-permute-start(f32[2,2,1536]{2,1,0:T(2,128)} %dynamic_update_slice.5), channel_id=1, source_target_pairs={{0,16},{16,0},{1,17},{17,1},{2,18},{18,2},{3,19},{19,3},{4,20},{20... | collective-permute-start | bytes 73736 | tf_op jit(solution)/shard_map/ppermute | solution.py:22
  43.5 33.1 %collective-permute-start.7 = (s32[1,128]{1,0:T(1,128)}, s32[1,128]{1,0:T(1,128)}, u32[]{:S(2)}, u32[]{:S(2)}) collective-permute-start(s32[1,128]{1,0:T(1,128)} %constant_dynamic-slice_fusion.2), channel_id=1, source_target_pairs={{0,4},{4,0},{1,5},{5,1},{2,6},{6,2},{3,7},{7,3},{8,12},{12,8},{9,1... | collective-permute-start | bytes 1544 | tf_op jit(solution)/shard_map/ppermute | solution.py:22
  47.1 66.3 %collective-permute-start.8 = (bf16[2,96,1536]{2,1,0:T(8,128)(2,1)}, bf16[2,96,1536]{2,1,0:T(8,128)(2,1)}, u32[]{:S(2)}, u32[]{:S(2)}) collective-permute-start(bf16[2,96,1536]{2,1,0:T(8,128)(2,1)} %all_gather.16), channel_id=1, source_target_pairs={{0,8},{8,0},{1,9},{9,1},{2,10},{10,2},{3,11},{11,3},{4,12},{12,4},... | collective-permute-start | bytes 1769480 | tf_op jit(solution)/shard_map/ppermute | solution.py:22
  60.8 81.3 %all-to-all-start.1 = ((bf16[8,96,1024]{2,1,0:T(8,128)(2,1)}), bf16[8,96,1024]{2,1,0:T(8,128)(2,1)S(1)}, u32[]{:S(2)}, u32[]{:S(2)}) async-start(bf16[8,96,1024]{2,1,0:T(8,128)(2,1)} %reshape.544), calls=%async_computation.1 | async-start | bytes 3145728 | tf_op jit(solution)/shard_map/all_to_all | solution.py:216
  64.4 77.7 %all-gather.11.cloned.1.call-start = ((), (), s32[]{:S(2)}) async-start(), calls=%async_computation.18 | async-start | bytes 1474560 | tf_op jit(solution)/shard_map/all_gather | solution.py:224
  67.4 58.4 %collective-permute-start.18 = (bf16[128,1536]{1,0:T(8,128)(2,1)}, bf16[128,1536]{1,0:T(8,128)(2,1)}, u32[]{:S(2)}, u32[]{:S(2)}) collective-permute-start(bf16[128,1536]{1,0:T(8,128)(2,1)} %bitcast.39), channel_id=1, source_target_pairs={{0,8},{8,0},{1,9},{9,1},{2,10},{10,2},{3,11},{11,3},{4,12},{12,4},... | collective-permute-start | bytes 1179656 | tf_op jit(solution)/shard_map/ppermute | solution.py:22
  69.4 207.7 %collective-permute-start.50 = (bf16[128,1536]{0,1:T(8,128)(2,1)S(1)}, bf16[128,1536]{0,1:T(8,128)(2,1)}, u32[]{:S(2)}, u32[]{:S(2)}) collective-permute-start(bf16[128,1536]{0,1:T(8,128)(2,1)S(1)} %bitcast.597), channel_id=1, source_target_pairs={{0,4},{4,0},{1,5},{5,1},{2,6},{6,2},{3,7},{7,3},{8,12},{12,8},{9,1... | collective-permute-start | bytes 1179656 | tf_op jit(solution)/shard_map/ppermute | solution.py:22
  76.5 34.4 %collective-permute-start.1 = (f32[2,2,1536]{2,1,0:T(2,128)}, f32[2,2,1536]{2,1,0:T(2,128)S(1)}, u32[]{:S(2)}, u32[]{:S(2)}) collective-permute-start(f32[2,2,1536]{2,1,0:T(2,128)} %add.444), channel_id=1, source_target_pairs={{0,4},{4,0},{1,5},{5,1},{2,6},{6,2},{3,7},{7,3},{8,12},{12,8},{9,1... | collective-permute-start | bytes 73736 | tf_op jit(solution)/shard_map/ppermute | solution.py:22
  115.4 165.6 %all-gather.9.cloned.1.call-start = ((), (), s32[]{:S(2)}) async-start(), calls=%async_computation.13 | async-start | bytes 2949120 | tf_op jit(solution)/shard_map/all_gather | solution.py:223
  117.4 34.5 %collective-permute-start.9 = (bf16[1536,768]{1,0:T(8,128)(2,1)}, bf16[1536,768]{1,0:T(8,128)(2,1)}, u32[]{:S(2)}, u32[]{:S(2)}) collective-permute-start(bf16[1536,768]{1,0:T(8,128)(2,1)} %all-gather.7.cloned.1.call-done), channel_id=1, source_target_pairs={{0,16},{16,0},{1,17},{17,1},{2,18},{18,2},{3,19},{19,3},{4,20},{20... | collective-permute-start | bytes 7077896 | tf_op jit(solution)/shard_map/ppermute | solution.py:22
  127.8 93.7 %collective-permute-start.29 = (bf16[2,96,768]{2,1,0:T(8,128)(2,1)}, bf16[2,96,768]{2,1,0:T(8,128)(2,1)}, u32[]{:S(2)}, u32[]{:S(2)}) collective-permute-start(bf16[2,96,768]{2,1,0:T(8,128)(2,1)} %get-tuple-element.129), channel_id=1, source_target_pairs={{0,8},{8,0},{1,9},{9,1},{2,10},{10,2},{3,11},{11,3},{4,12},{12,4},... | collective-permute-start | bytes 884744 | tf_op jit(solution)/shard_map/ppermute | solution.py:22
  142.1 19.4 %collective-permute-start.10 = (bf16[384,1536]{1,0:T(8,128)(2,1)}, bf16[384,1536]{1,0:T(8,128)(2,1)}, u32[]{:S(2)}, u32[]{:S(2)}) collective-permute-start(bf16[384,1536]{1,0:T(8,128)(2,1)} %bitcast.632), channel_id=1, source_target_pairs={{0,16},{16,0},{1,17},{17,1},{2,18},{18,2},{3,19},{19,3},{4,20},{20... | collective-permute-start | bytes 3538952 | tf_op jit(solution)/shard_map/ppermute | solution.py:22
  143.5 38.1 %collective-permute-start.16 = (bf16[2,2,96,1024]{3,2,1,0:T(8,128)(2,1)}, bf16[2,2,96,1024]{3,2,1,0:T(8,128)(2,1)}, u32[]{:S(2)}, u32[]{:S(2)}) collective-permute-start(bf16[2,2,96,1024]{3,2,1,0:T(8,128)(2,1)} %bitcast.32), channel_id=1, source_target_pairs={{0,8},{8,0},{1,9},{9,1},{2,10},{10,2},{3,11},{11,3},{4,12},{12,4},... | collective-permute-start | bytes 2359304 | tf_op jit(solution)/shard_map/ppermute | solution.py:22
  164.2 25.7 %collective-permute-start.11 = (bf16[128,1536]{1,0:T(8,128)(2,1)S(1)}, bf16[128,1536]{1,0:T(8,128)(2,1)S(1)}, u32[]{:S(2)}, u32[]{:S(2)}) collective-permute-start(bf16[128,1536]{1,0:T(8,128)(2,1)S(1)} %slice.1046), channel_id=1, source_target_pairs={{0,4},{4,0},{1,5},{5,1},{2,6},{6,2},{3,7},{7,3},{8,12},{12,8},{9,1... | collective-permute-start | bytes 1179656 | tf_op jit(solution)/shard_map/ppermute | solution.py:22
  184.4 66.1 %collective-permute-start.20 = (bf16[768,1024]{1,0:T(8,128)(2,1)}, bf16[768,1024]{1,0:T(8,128)(2,1)}, u32[]{:S(2)}, u32[]{:S(2)}) collective-permute-start(bf16[768,1024]{1,0:T(8,128)(2,1)} %bitcast.36), channel_id=1, source_target_pairs={{0,16},{16,0},{1,17},{17,1},{2,18},{18,2},{3,19},{19,3},{4,20},{20... | collective-permute-start | bytes 4718600 | tf_op jit(solution)/shard_map/ppermute | solution.py:22
  184.4 37.1 %collective-permute-start.17 = (bf16[768,1024]{1,0:T(8,128)(2,1)}, bf16[768,1024]{1,0:T(8,128)(2,1)}, u32[]{:S(2)}, u32[]{:S(2)}) collective-permute-start(bf16[768,1024]{1,0:T(8,128)(2,1)} %bitcast.36), channel_id=1, source_target_pairs={{0,1},{1,0},{2,3},{3,2},{4,5},{5,4},{6,7},{7,6},{8,9},{9,8},{10,11... | collective-permute-start | bytes 4718600 | tf_op jit(solution)/shard_map/ppermute | solution.py:22
  191.4 33.0 %collective-permute-start.12 = (bf16[128,1536]{1,0:T(8,128)(2,1)}, bf16[128,1536]{1,0:T(8,128)(2,1)S(1)}, u32[]{:S(2)}, u32[]{:S(2)}) collective-permute-start(bf16[128,1536]{1,0:T(8,128)(2,1)} %get-tuple-element.68), channel_id=1, source_target_pairs={{0,2},{2,0},{1,3},{3,1},{4,6},{6,4},{5,7},{7,5},{8,10},{10,8},{9,1... | collective-permute-start | bytes 1179656 | tf_op jit(solution)/shard_map/ppermute | solution.py:22
  221.5 32.1 %collective-permute-start.21 = (bf16[768,1024]{1,0:T(8,128)(2,1)}, bf16[768,1024]{1,0:T(8,128)(2,1)}, u32[]{:S(2)}, u32[]{:S(2)}) collective-permute-start(bf16[768,1024]{1,0:T(8,128)(2,1)} %collective-permute-done.17), channel_id=1, source_target_pairs={{0,16},{16,0},{1,17},{17,1},{2,18},{18,2},{3,19},{19,3},{4,20},{20... | collective-permute-start | bytes 4718600 | tf_op jit(solution)/shard_map/ppermute | solution.py:22
  223.8 85.5 %all-gather.13.cloned.1.call-start = ((), (), s32[]{:S(2)}) async-start(), calls=%async_computation.19 | async-start | bytes 1474560 | tf_op jit(solution)/shard_map/all_gather | solution.py:224
  224.4 26.1 %collective-permute-start.19 = (bf16[256,1536]{1,0:T(8,128)(2,1)S(1)}, bf16[256,1536]{1,0:T(8,128)(2,1)S(1)}, u32[]{:S(2)}, u32[]{:S(2)}) collective-permute-start(bf16[256,1536]{1,0:T(8,128)(2,1)S(1)} %bitcast.584), channel_id=1, source_target_pairs={{0,1},{1,0},{2,3},{3,2},{4,5},{5,4},{6,7},{7,6},{8,9},{9,8},{10,11... | collective-permute-start | bytes 2359304 | tf_op jit(solution)/shard_map/ppermute | solution.py:22
  245.4 33.5 %collective-permute-start.49 = (bf16[128,1536]{0,1:T(8,128)(2,1)S(1)}, bf16[128,1536]{0,1:T(8,128)(2,1)}, u32[]{:S(2)}, u32[]{:S(2)}) collective-permute-start(bf16[128,1536]{0,1:T(8,128)(2,1)S(1)} %bitcast.598), channel_id=1, source_target_pairs={{0,2},{2,0},{1,3},{3,1},{4,6},{6,4},{5,7},{7,5},{8,10},{10,8},{9,1... | collective-permute-start | bytes 1179656 | tf_op jit(solution)/shard_map/ppermute | solution.py:22
  271.9 20.1 %collective-permute-start.39 = (bf16[128,1536]{1,0:T(8,128)(2,1)S(1)}, bf16[128,1536]{1,0:T(8,128)(2,1)S(1)}, u32[]{:S(2)}, u32[]{:S(2)}) collective-permute-start(bf16[128,1536]{1,0:T(8,128)(2,1)S(1)} %bitcast.627), channel_id=1, source_target_pairs={{0,8},{8,0},{1,9},{9,1},{2,10},{10,2},{3,11},{11,3},{4,12},{12,4},... | collective-permute-start | bytes 1179656 | tf_op jit(solution)/shard_map/ppermute | solution.py:22
  281.0 78.2 %collective-permute-start.30 = (bf16[1536,768]{1,0:T(8,128)(2,1)}, bf16[1536,768]{1,0:T(8,128)(2,1)}, u32[]{:S(2)}, u32[]{:S(2)}) collective-permute-start(bf16[1536,768]{1,0:T(8,128)(2,1)} %all-gather.9.cloned.1.call-done), channel_id=1, source_target_pairs={{0,16},{16,0},{1,17},{17,1},{2,18},{18,2},{3,19},{19,3},{4,20},{20... | collective-permute-start | bytes 7077896 | tf_op jit(solution)/shard_map/ppermute | solution.py:22
  283.1 26.3 %collective-permute-start.25 = (bf16[128,1536]{1,0:T(8,128)(2,1)}, bf16[128,1536]{1,0:T(8,128)(2,1)}, u32[]{:S(2)}, u32[]{:S(2)}) collective-permute-start(bf16[128,1536]{1,0:T(8,128)(2,1)} %pad_maximum_fusion.20), channel_id=1, source_target_pairs={{0,2},{2,0},{1,3},{3,1},{4,6},{6,4},{5,7},{7,5},{8,10},{10,8},{9,1... | collective-permute-start | bytes 1179656 | tf_op jit(solution)/shard_map/ppermute | solution.py:22
  293.6 88.5 %collective-permute-start.40 = (bf16[256,1536]{1,0:T(8,128)(2,1)}, bf16[256,1536]{1,0:T(8,128)(2,1)}, u32[]{:S(2)}, u32[]{:S(2)}) collective-permute-start(bf16[256,1536]{1,0:T(8,128)(2,1)} %bitcast.69), channel_id=1, source_target_pairs={{0,1},{1,0},{2,3},{3,2},{4,5},{5,4},{6,7},{7,6},{8,9},{9,8},{10,11... | collective-permute-start | bytes 2359304 | tf_op jit(solution)/shard_map/ppermute | solution.py:22
  294.4 101.8 %collective-permute-start.43 = (bf16[256,1536]{1,0:T(8,128)(2,1)}, bf16[256,1536]{1,0:T(8,128)(2,1)}, u32[]{:S(2)}, u32[]{:S(2)}) collective-permute-start(bf16[256,1536]{1,0:T(8,128)(2,1)} %bitcast.69), channel_id=1, source_target_pairs={{0,16},{16,0},{1,17},{17,1},{2,18},{18,2},{3,19},{19,3},{4,20},{20... | collective-permute-start | bytes 2359304 | tf_op jit(solution)/shard_map/ppermute | solution.py:22
  309.3 66.3 %collective-permute-start.31 = (bf16[384,1536]{1,0:T(8,128)(2,1)}, bf16[384,1536]{1,0:T(8,128)(2,1)}, u32[]{:S(2)}, u32[]{:S(2)}) collective-permute-start(bf16[384,1536]{1,0:T(8,128)(2,1)} %bitcast.633), channel_id=1, source_target_pairs={{0,16},{16,0},{1,17},{17,1},{2,18},{18,2},{3,19},{19,3},{4,20},{20... | collective-permute-start | bytes 3538952 | tf_op jit(solution)/shard_map/ppermute | solution.py:22
  309.3 37.7 %collective-permute-start.37 = (bf16[2,2,96,1024]{3,2,1,0:T(8,128)(2,1)S(1)}, bf16[2,2,96,1024]{3,2,1,0:T(8,128)(2,1)S(1)}, u32[]{:S(2)}, u32[]{:S(2)}) collective-permute-start(bf16[2,2,96,1024]{3,2,1,0:T(8,128)(2,1)S(1)} %bitcast.613), channel_id=1, source_target_pairs={{0,8},{8,0},{1,9},{9,1},{2,10},{10,2},{3,11},{11,3},{4,12},{12,4},... | collective-permute-start | bytes 2359304 | tf_op jit(solution)/shard_map/ppermute | solution.py:22
  357.6 35.3 %collective-permute-start.38 = (bf16[768,1024]{1,0:T(8,128)(2,1)}, bf16[768,1024]{1,0:T(8,128)(2,1)}, u32[]{:S(2)}, u32[]{:S(2)}) collective-permute-start(bf16[768,1024]{1,0:T(8,128)(2,1)} %bitcast.65), channel_id=1, source_target_pairs={{0,1},{1,0},{2,3},{3,2},{4,5},{5,4},{6,7},{7,6},{8,9},{9,8},{10,11... | collective-permute-start | bytes 4718600 | tf_op jit(solution)/shard_map/ppermute | solution.py:22
  384.6 31.7 %collective-permute-start.41 = (bf16[768,1024]{1,0:T(8,128)(2,1)}, bf16[768,1024]{1,0:T(8,128)(2,1)}, u32[]{:S(2)}, u32[]{:S(2)}) collective-permute-start(bf16[768,1024]{1,0:T(8,128)(2,1)} %bitcast.65), channel_id=1, source_target_pairs={{0,16},{16,0},{1,17},{17,1},{2,18},{18,2},{3,19},{19,3},{4,20},{20... | collective-permute-start | bytes 4718600 | tf_op jit(solution)/shard_map/ppermute | solution.py:22
  393.0 26.1 %collective-permute-start.42 = (bf16[768,1024]{1,0:T(8,128)(2,1)}, bf16[768,1024]{1,0:T(8,128)(2,1)}, u32[]{:S(2)}, u32[]{:S(2)}) collective-permute-start(bf16[768,1024]{1,0:T(8,128)(2,1)} %collective-permute-done.38), channel_id=1, source_target_pairs={{0,16},{16,0},{1,17},{17,1},{2,18},{18,2},{3,19},{19,3},{4,20},{20... | collective-permute-start | bytes 4718600 | tf_op jit(solution)/shard_map/ppermute | solution.py:22
  438.4 21.8 %collective-permute-start.45 = (bf16[64,1536]{1,0:T(8,128)(2,1)S(1)}, bf16[64,1536]{1,0:T(8,128)(2,1)S(1)}, u32[]{:S(2)}, u32[]{:S(2)}) collective-permute-start(bf16[64,1536]{1,0:T(8,128)(2,1)S(1)} %get-tuple-element.97), channel_id=1, source_target_pairs={{0,4},{4,0},{1,5},{5,1},{2,6},{6,2},{3,7},{7,3},{8,12},{12,8},{9,1... | collective-permute-start | bytes 589832 | tf_op jit(solution)/shard_map/ppermute | solution.py:22
  439.4 21.2 %collective-permute-start.47 = (bf16[64,1536]{1,0:T(8,128)(2,1)S(1)}, bf16[64,1536]{1,0:T(8,128)(2,1)S(1)}, u32[]{:S(2)}, u32[]{:S(2)}) collective-permute-start(bf16[64,1536]{1,0:T(8,128)(2,1)S(1)} %get-tuple-element.98), channel_id=1, source_target_pairs={{0,2},{2,0},{1,3},{3,1},{4,6},{6,4},{5,7},{7,5},{8,10},{10,8},{9,1... | collective-permute-start | bytes 589832 | tf_op jit(solution)/shard_map/ppermute | solution.py:22
  454.7 38.3 %collective-permute-start.96 = (bf16[256,1536]{1,0:T(8,128)(2,1)}, bf16[256,1536]{1,0:T(8,128)(2,1)}, u32[]{:S(2)}, u32[]{:S(2)}) collective-permute-start(bf16[256,1536]{1,0:T(8,128)(2,1)} %convolution_convert_fusion.4), channel_id=1, source_target_pairs={{0,16},{16,0},{1,17},{17,1},{2,18},{18,2},{3,19},{19,3},{4,20},{20... | collective-permute-start | bytes 2359304 | tf_op jit(solution)/shard_map/ppermute | solution.py:22
  458.9 88.5 %collective-permute-start.95 = (bf16[256,1536]{1,0:T(8,128)(2,1)}, bf16[256,1536]{1,0:T(8,128)(2,1)}, u32[]{:S(2)}, u32[]{:S(2)}) collective-permute-start(bf16[256,1536]{1,0:T(8,128)(2,1)} %convolution_convert_fusion.5), channel_id=1, source_target_pairs={{0,16},{16,0},{1,17},{17,1},{2,18},{18,2},{3,19},{19,3},{4,20},{20... | collective-permute-start | bytes 2359304 | tf_op jit(solution)/shard_map/ppermute | solution.py:22
  460.1 76.8 %collective-permute-start.87 = (bf16[768,1024]{1,0:T(8,128)(2,1)}, bf16[768,1024]{1,0:T(8,128)(2,1)}, u32[]{:S(2)}, u32[]{:S(2)}) collective-permute-start(bf16[768,1024]{1,0:T(8,128)(2,1)} %convolution_convert_fusion.9), channel_id=1, source_target_pairs={{0,16},{16,0},{1,17},{17,1},{2,18},{18,2},{3,19},{19,3},{4,20},{20... | collective-permute-start | bytes 4718600 | tf_op jit(solution)/shard_map/ppermute | solution.py:22
  482.5 59.5 %collective-permute-start.88 = (bf16[768,1024]{1,0:T(8,128)(2,1)}, bf16[768,1024]{1,0:T(8,128)(2,1)}, u32[]{:S(2)}, u32[]{:S(2)}) collective-permute-start(bf16[768,1024]{1,0:T(8,128)(2,1)} %convolution_convert_fusion.8), channel_id=1, source_target_pairs={{0,16},{16,0},{1,17},{17,1},{2,18},{18,2},{3,19},{19,3},{4,20},{20... | collective-permute-start | bytes 4718600 | tf_op jit(solution)/shard_map/ppermute | solution.py:22
  488.7 309.2 %all-to-all-start.3 = ((bf16[2,128,1536]{1,2,0:T(8,128)(2,1)}), bf16[2,128,1536]{1,2,0:T(8,128)(2,1)}, u32[]{:S(2)}, u32[]{:S(2)}) async-start(bf16[2,128,1536]{1,2,0:T(8,128)(2,1)} %bitcast.603), calls=%async_computation.3 | async-start | bytes 1572864 | tf_op jit(solution)/shard_map/all_to_all | solution.py:332
  493.0 321.9 %reduce-scatter.11.cloned.1.call-start = ((), (), s32[]{:S(2)}) async-start(), calls=%async_computation.17 | async-start | bytes 1474560 | tf_op jit(solution)/shard_map/reduce_scatter | solution.py:312
  495.7 52.7 %collective-permute-start.97 = (bf16[256,1536]{1,0:T(8,128)(2,1)}, bf16[256,1536]{1,0:T(8,128)(2,1)}, u32[]{:S(2)}, u32[]{:S(2)}) collective-permute-start(bf16[256,1536]{1,0:T(8,128)(2,1)} %fusion.13), channel_id=1, source_target_pairs={{0,1},{1,0},{2,3},{3,2},{4,5},{5,4},{6,7},{7,6},{8,9},{9,8},{10,11... | collective-permute-start | bytes 2359304 | tf_op jit(solution)/shard_map/ppermute | solution.py:22
  532.0 90.8 %collective-permute-start.80 = (bf16[384,1536]{1,0:T(8,128)(2,1)}, bf16[384,1536]{1,0:T(8,128)(2,1)}, u32[]{:S(2)}, u32[]{:S(2)}) collective-permute-start(bf16[384,1536]{1,0:T(8,128)(2,1)} %convolution_convert_fusion.2), channel_id=1, source_target_pairs={{0,16},{16,0},{1,17},{17,1},{2,18},{18,2},{3,19},{19,3},{4,20},{20... | collective-permute-start | bytes 3538952 | tf_op jit(solution)/shard_map/ppermute | solution.py:22
  536.9 123.2 %collective-permute-start.76 = (bf16[1536,768]{1,0:T(8,128)(2,1)}, bf16[1536,768]{1,0:T(8,128)(2,1)}, u32[]{:S(2)}, u32[]{:S(2)}) collective-permute-start(bf16[1536,768]{1,0:T(8,128)(2,1)} %convolution_convert_fusion), channel_id=1, source_target_pairs={{0,16},{16,0},{1,17},{17,1},{2,18},{18,2},{3,19},{19,3},{4,20},{20... | collective-permute-start | bytes 7077896 | tf_op jit(solution)/shard_map/ppermute | solution.py:22
  548.5 126.0 %collective-permute-start.89 = (bf16[768,1024]{1,0:T(8,128)(2,1)}, bf16[768,1024]{1,0:T(8,128)(2,1)}, u32[]{:S(2)}, u32[]{:S(2)}) collective-permute-start(bf16[768,1024]{1,0:T(8,128)(2,1)} %add_convert_fusion.3), channel_id=1, source_target_pairs={{0,1},{1,0},{2,3},{3,2},{4,5},{5,4},{6,7},{7,6},{8,9},{9,8},{10,11... | collective-permute-start | bytes 4718600 | tf_op jit(solution)/shard_map/ppermute | solution.py:22
  618.8 87.6 %collective-permute-start.91 = (bf16[256,1536]{1,0:T(8,128)(2,1)}, bf16[256,1536]{1,0:T(8,128)(2,1)}, u32[]{:S(2)}, u32[]{:S(2)}) collective-permute-start(bf16[256,1536]{1,0:T(8,128)(2,1)} %convolution_convert_fusion.7), channel_id=1, source_target_pairs={{0,16},{16,0},{1,17},{17,1},{2,18},{18,2},{3,19},{19,3},{4,20},{20... | collective-permute-start | bytes 2359304 | tf_op jit(solution)/shard_map/ppermute | solution.py:22
  627.6 224.9 %reduce-scatter.9.cloned.1.call-start = ((), (), s32[]{:S(2)}) async-start(), calls=%async_computation.16 | async-start | bytes 1474560 | tf_op jit(solution)/shard_map/reduce_scatter | solution.py:312
  627.7 91.1 %collective-permute-start.83 = (bf16[768,1024]{1,0:T(8,128)(2,1)}, bf16[768,1024]{1,0:T(8,128)(2,1)}, u32[]{:S(2)}, u32[]{:S(2)}) collective-permute-start(bf16[768,1024]{1,0:T(8,128)(2,1)} %convolution_convert_fusion.11), channel_id=1, source_target_pairs={{0,16},{16,0},{1,17},{17,1},{2,18},{18,2},{3,19},{19,3},{4,20},{20... | collective-permute-start | bytes 4718600 | tf_op jit(solution)/shard_map/ppermute | solution.py:22
  648.2 43.6 %collective-permute-start.84 = (bf16[768,1024]{1,0:T(8,128)(2,1)}, bf16[768,1024]{1,0:T(8,128)(2,1)}, u32[]{:S(2)}, u32[]{:S(2)}) collective-permute-start(bf16[768,1024]{1,0:T(8,128)(2,1)} %convolution_convert_fusion.10), channel_id=1, source_target_pairs={{0,16},{16,0},{1,17},{17,1},{2,18},{18,2},{3,19},{19,3},{4,20},{20... | collective-permute-start | bytes 4718600 | tf_op jit(solution)/shard_map/ppermute | solution.py:22
  651.7 204.2 %reduce-scatter.7.cloned.1.call-start = ((), (), s32[]{:S(2)}) async-start(), calls=%async_computation.15 | async-start | bytes 2949120 | tf_op jit(solution)/shard_map/reduce_scatter | solution.py:318
  664.1 194.3 %reduce-scatter.5.cloned.1.call-start = ((), (), s32[]{:S(2)}) async-start(), calls=%async_computation.14 | async-start | bytes 2949120 | tf_op jit(solution)/shard_map/reduce_scatter | solution.py:318
  669.1 30.1 %collective-permute-start.74 = (bf16[1536,768]{1,0:T(8,128)(2,1)}, bf16[1536,768]{1,0:T(8,128)(2,1)}, u32[]{:S(2)}, u32[]{:S(2)}) collective-permute-start(bf16[1536,768]{1,0:T(8,128)(2,1)} %convolution_convert_fusion.1), channel_id=1, source_target_pairs={{0,16},{16,0},{1,17},{17,1},{2,18},{18,2},{3,19},{19,3},{4,20},{20... | collective-permute-start | bytes 7077896 | tf_op jit(solution)/shard_map/ppermute | solution.py:22
  685.7 26.6 %collective-permute-start.93 = (bf16[256,1536]{1,0:T(8,128)(2,1)}, bf16[256,1536]{1,0:T(8,128)(2,1)}, u32[]{:S(2)}, u32[]{:S(2)}) collective-permute-start(bf16[256,1536]{1,0:T(8,128)(2,1)} %fusion.8), channel_id=1, source_target_pairs={{0,1},{1,0},{2,3},{3,2},{4,5},{5,4},{6,7},{7,6},{8,9},{9,8},{10,11... | collective-permute-start | bytes 2359304 | tf_op jit(solution)/shard_map/ppermute | solution.py:22
  691.8 72.5 %collective-permute-start.90 = (bf16[2,2,96,1024]{3,2,1,0:T(8,128)(2,1)}, bf16[2,2,96,1024]{3,2,1,0:T(8,128)(2,1)}, u32[]{:S(2)}, u32[]{:S(2)}) collective-permute-start(bf16[2,2,96,1024]{3,2,1,0:T(8,128)(2,1)} %dynamic-slice_bitcast_fusion), channel_id=1, source_target_pairs={{0,8},{8,0},{1,9},{9,1},{2,10},{10,2},{3,11},{11,3},{4,12},{12,4},... | collective-permute-start | bytes 2359304 | tf_op jit(solution)/shard_map/ppermute | solution.py:22
  699.2 58.4 %collective-permute-start.85 = (bf16[768,1024]{1,0:T(8,128)(2,1)}, bf16[768,1024]{1,0:T(8,128)(2,1)}, u32[]{:S(2)}, u32[]{:S(2)}) collective-permute-start(bf16[768,1024]{1,0:T(8,128)(2,1)} %add_convert_fusion.6), channel_id=1, source_target_pairs={{0,1},{1,0},{2,3},{3,2},{4,5},{5,4},{6,7},{7,6},{8,9},{9,8},{10,11... | collective-permute-start | bytes 4718600 | tf_op jit(solution)/shard_map/ppermute | solution.py:22
  706.4 105.7 %collective-permute-start.69 = (f32[2,2,1536]{2,1,0:T(2,128)}, f32[2,2,1536]{2,1,0:T(2,128)}, u32[]{:S(2)}, u32[]{:S(2)}) collective-permute-start(f32[2,2,1536]{2,1,0:T(2,128)} %pad_maximum_fusion.36), channel_id=1, source_target_pairs={{0,16},{16,0},{1,17},{17,1},{2,18},{18,2},{3,19},{19,3},{4,20},{20... | collective-permute-start | bytes 73736 | tf_op jit(solution)/shard_map/ppermute | solution.py:22
  714.4 48.9 %collective-permute-start.94 = (bf16[128,1536]{1,0:T(8,128)(2,1)S(1)}, bf16[128,1536]{1,0:T(8,128)(2,1)S(1)}, u32[]{:S(2)}, u32[]{:S(2)}) collective-permute-start(bf16[128,1536]{1,0:T(8,128)(2,1)S(1)} %dynamic-slice_bitcast_fusion.3), channel_id=1, source_target_pairs={{0,8},{8,0},{1,9},{9,1},{2,10},{10,2},{3,11},{11,3},{4,12},{12,4},... | collective-permute-start | bytes 1179656 | tf_op jit(solution)/shard_map/ppermute | solution.py:22
  759.7 36.5 %collective-permute-start.86 = (bf16[2,2,96,1024]{3,2,1,0:T(8,128)(2,1)S(1)}, bf16[2,2,96,1024]{3,2,1,0:T(8,128)(2,1)S(1)}, u32[]{:S(2)}, u32[]{:S(2)}) collective-permute-start(bf16[2,2,96,1024]{3,2,1,0:T(8,128)(2,1)S(1)} %dynamic-slice_bitcast_fusion.1), channel_id=1, source_target_pairs={{0,8},{8,0},{1,9},{9,1},{2,10},{10,2},{3,11},{11,3},{4,12},{12,4},... | collective-permute-start | bytes 2359304 | tf_op jit(solution)/shard_map/ppermute | solution.py:22
  808.1 83.6 %all-to-all-start.6 = ((bf16[8,96,1024]{2,1,0:T(8,128)(2,1)}), bf16[8,96,1024]{2,1,0:T(8,128)(2,1)S(1)}, u32[]{:S(2)}, u32[]{:S(2)}) async-start(bf16[8,96,1024]{2,1,0:T(8,128)(2,1)} %bitcast.156), calls=%async_computation.10 | async-start | bytes 3145728 | tf_op jit(solution)/shard_map/all_to_all | solution.py:352
  812.8 26.0 %collective-permute-start.70 = (f32[2,2,1536]{2,1,0:T(2,128)S(1)}, f32[2,2,1536]{2,1,0:T(2,128)S(1)}, u32[]{:S(2)}, u32[]{:S(2)}) collective-permute-start(f32[2,2,1536]{2,1,0:T(2,128)S(1)} %fusion.192), channel_id=1, source_target_pairs={{0,4},{4,0},{1,5},{5,1},{2,6},{6,2},{3,7},{7,3},{8,12},{12,8},{9,1... | collective-permute-start | bytes 73736 | tf_op jit(solution)/shard_map/ppermute | solution.py:22
  814.9 39.9 %collective-permute-start.81 = (bf16[96,1536]{1,0:T(8,128)(2,1)}, bf16[96,1536]{1,0:T(8,128)(2,1)}, u32[]{:S(2)}, u32[]{:S(2)}) collective-permute-start(bf16[96,1536]{1,0:T(8,128)(2,1)} %reduce-scatter.11.cloned.1.call-done), channel_id=1, source_target_pairs={{0,8},{8,0},{1,9},{9,1},{2,10},{10,2},{3,11},{11,3},{4,12},{12,4},... | collective-permute-start | bytes 884744 | tf_op jit(solution)/shard_map/ppermute | solution.py:22
  852.5 27.6 %collective-permute-start.79 = (bf16[96,1536]{1,0:T(8,128)(2,1)}, bf16[96,1536]{1,0:T(8,128)(2,1)S(1)}, u32[]{:S(2)}, u32[]{:S(2)}) collective-permute-start(bf16[96,1536]{1,0:T(8,128)(2,1)} %reduce-scatter.9.cloned.1.call-done), channel_id=1, source_target_pairs={{0,8},{8,0},{1,9},{9,1},{2,10},{10,2},{3,11},{11,3},{4,12},{12,4},... | collective-permute-start | bytes 884744 | tf_op jit(solution)/shard_map/ppermute | solution.py:22
  857.6 28.9 %collective-permute-start.77 = (bf16[2,96,768]{2,1,0:T(8,128)(2,1)}, bf16[2,96,768]{2,1,0:T(8,128)(2,1)}, u32[]{:S(2)}, u32[]{:S(2)}) collective-permute-start(bf16[2,96,768]{2,1,0:T(8,128)(2,1)} %dynamic-slice_bitcast_fusion.4), channel_id=1, source_target_pairs={{0,8},{8,0},{1,9},{9,1},{2,10},{10,2},{3,11},{11,3},{4,12},{12,4},... | collective-permute-start | bytes 884744 | tf_op jit(solution)/shard_map/ppermute | solution.py:22
  859.5 31.3 %collective-permute-start.75 = (bf16[2,96,768]{2,1,0:T(8,128)(2,1)S(1)}, bf16[2,96,768]{2,1,0:T(8,128)(2,1)S(1)}, u32[]{:S(2)}, u32[]{:S(2)}) collective-permute-start(bf16[2,96,768]{2,1,0:T(8,128)(2,1)S(1)} %dynamic-slice_bitcast_fusion.5), channel_id=1, source_target_pairs={{0,8},{8,0},{1,9},{9,1},{2,10},{10,2},{3,11},{11,3},{4,12},{12,4},... | collective-permute-start | bytes 884744 | tf_op jit(solution)/shard_map/ppermute | solution.py:22
  891.7 25.7 %all-to-all-start.5 = ((bf16[4,96,768]{2,1,0:T(8,128)(2,1)}), bf16[4,96,768]{2,1,0:T(8,128)(2,1)}, u32[]{:S(2)}, u32[]{:S(2)}) async-start(bf16[4,96,768]{2,1,0:T(8,128)(2,1)} %bitcast.138), calls=%async_computation.7 | async-start | bytes 1179648 | tf_op jit(solution)/shard_map/all_to_all | solution.py:342
  (278 other events, 2432.4 us)
Sparse Core Ops, SparseCore 0:
  41.2 46.0 all-gather.6
  115.5 26.5 all-gather.10
  224.0 43.5 all-gather.8
  271.8 37.4 all-gather.12
  627.7 29.1 reduce-scatter.10
  660.3 28.6 reduce-scatter.8
  692.6 56.4 reduce-scatter.6
  752.2 37.3 reduce-scatter.4
